TPU v7x, 512 devices: a whole 4x4x16 slice. The times are simulated.
512 devices in a mesh: req: 64 (over y, z), tensor: 8 (over x, core).
Axes of the slice: x: 4, y: 4, z: 16, core: 2. Of those that a mesh axis runs over, the one named last changes fastest.
Arguments:
- pre_tokens: bfloat16 [16384, 1024], P('req', 'tensor'), may hold values from -24 to 24
- dec_tokens: bfloat16 [64, 1024], P('req', 'tensor'), may hold values from -24 to 24
- req_of: int32 [64], replicated, may hold values from 0 to 63, each once
- page_table: int32 [64, 16], replicated, may hold values from -1 to 575, as said below
- page_place: int32 [576], replicated, may hold values from 0 to 575, as said below
- cache_lengths: int32 [64], replicated, may hold values from 1 to 2048, as said below
- cache_keys: bfloat16 [576, 128, 1024], P('req', None, 'tensor'), may hold values from -24 to 24
- cache_values: bfloat16 [576, 128, 1024], P('req', None, 'tensor'), may hold values from -6 to 6
- w_qkv: bfloat16 [1024, 3, 1024], P(None, None, 'tensor'), may hold values from -0.1875 to 0.1875
- w_out: bfloat16 [1024, 1024], P('tensor'), may hold values from -0.1875 to 0.1875
- ln1_gain: float32 [1024], replicated, may hold values from 0.5 to 1.5
- ln1_bias: float32 [1024], replicated, may hold values from -1 to 1
- w_up: bfloat16 [1024, 4096], P(None, 'tensor'), may hold values from -0.1875 to 0.1875
- w_down: bfloat16 [4096, 1024], P('tensor'), may hold values from -0.09375 to 0.09375
- ln2_gain: float32 [1024], replicated, may hold values from 0.5 to 1.5
- ln2_bias: float32 [1024], replicated, may hold values from -1 to 1
Outputs:
- pre_out: bfloat16 [16384, 1024], P('req', 'tensor')
- dec_out: bfloat16 [64, 1024], P('req', 'tensor')
Inputs may be any that keep to these rules, and one draw needn't show every extreme that they name: `page_table`: entry j of row r is a page id for j < ceil(cache_lengths[r] / 128) and -1 after; no page id appears twice; the requests hold 544 pages together. `page_place`: a permutation; page p sits on index page_place[p] // 9 of req; one index of req holds at most 1 pages of one request, and some holds exactly 1. `cache_lengths`: some request has exactly 2048 tokens.
All inputs are finite; a program needn't handle non-finite values.
Results may differ from a plain program's by a relative error of at most 0.023.
Values may be sent and summed in bfloat16 or wider, within the bound.
A program may use at most 64 MiB of HBM per device.

v0:
```python
import math

import jax
import jax.numpy as jnp
from jax import lax
from jax.sharding import PartitionSpec as P

HD = 64


norm_eps = 1e-05
neg_large = -1e30


def norm_rows(total, gain, shift):
    mean = jnp.mean(total, axis=-1, keepdims=True)
    centered = total - mean
    var = jnp.mean(centered * centered, axis=-1, keepdims=True)
    return centered * lax.rsqrt(var + norm_eps) * gain + shift


def partial_softmax(query, keys, values, usable, scale):
    scores = jnp.einsum("bhd,bkhd->bhk", query, keys, preferred_element_type=jnp.float32) * scale
    scores = jnp.where(usable[:, None, :], scores, neg_large)
    top = jnp.max(scores, axis=-1)
    weights = jnp.where(usable[:, None, :], jnp.exp(scores - top[..., None]), 0.0)
    total = jnp.sum(weights, axis=-1)
    summed = jnp.einsum(
        "bhk,bkhd->bhd", weights.astype(jnp.bfloat16), values, preferred_element_type=jnp.float32
    )
    return (top, total, summed)


def finish_context(top, total, summed, own_query, own_key, own_value, scale):
    own_score = (
        jnp.sum(own_query.astype(jnp.float32) * own_key.astype(jnp.float32), axis=-1) * scale
    )
    best = jnp.maximum(top, own_score)
    old_factor = jnp.exp(top - best)
    own_weight = jnp.exp(own_score - best)
    own_short = lax.optimization_barrier(own_weight.astype(jnp.bfloat16)).astype(jnp.float32)
    numer = summed * old_factor[:, None] + own_short[:, None] * own_value.astype(jnp.float32)
    return (numer / (total * old_factor + own_weight)[:, None]).astype(jnp.bfloat16)


def local(
    pre_tokens,
    dec_tokens,
    req_of,
    page_table,
    page_place,
    cache_lengths,
    cache_keys,
    cache_values,
    w_qkv,
    w_out,
    ln1_gain,
    ln1_bias,
    w_up,
    w_down,
    ln2_gain,
    ln2_bias,
):
    pre_len = pre_tokens.shape[0]
    width = w_qkv.shape[0]
    cols = w_qkv.shape[2]
    heads_here = cols // HD
    scale = 1.0 / math.sqrt(HD)
    local_rows = jnp.concatenate([pre_tokens, dec_tokens], axis=0)
    full_rows = lax.all_gather(local_rows, "tensor", axis=1, tiled=True)
    mixed = jnp.dot(
        full_rows, w_qkv.reshape(width, 3 * cols), preferred_element_type=jnp.float32
    ).astype(jnp.bfloat16)
    mixed = mixed.reshape(pre_len + 1, 3, heads_here, HD)
    queries = mixed[:, 0]
    keys_new = mixed[:, 1]
    values_new = mixed[:, 2]
    scores = (
        jnp.einsum(
            "qhd,khd->hqk",
            queries[:pre_len],
            keys_new[:pre_len],
            preferred_element_type=jnp.float32,
        )
        * scale
    )
    row_pos = jnp.arange(pre_len, dtype=jnp.int32)
    causal = row_pos[:, None] >= row_pos[None, :]
    scores = jnp.where(causal[None], scores, neg_large)
    top = jnp.max(scores, axis=-1, keepdims=True)
    weights = jnp.where(causal[None], jnp.exp(scores - top), 0.0)
    total = jnp.sum(weights, axis=-1)
    pre_context = jnp.einsum(
        "hqk,khd->qhd",
        weights.astype(jnp.bfloat16),
        values_new[:pre_len],
        preferred_element_type=jnp.float32,
    )
    pre_context = (
        (pre_context / jnp.transpose(total)[:, :, None]).astype(jnp.bfloat16).reshape(pre_len, cols)
    )
    own_query = queries[pre_len]
    own_key = keys_new[pre_len]
    own_value = values_new[pre_len]
    me = lax.axis_index("req")
    n_req = lax.axis_size("req")
    pages_here = cache_keys.shape[0]
    page_len = cache_keys.shape[1]
    max_pages = page_table.shape[1]
    valid = page_table >= 0
    slots = page_place[jnp.maximum(page_table, 0)]
    holder = slots // pages_here
    local_slot = slots % pages_here
    page_ids = jnp.arange(max_pages, dtype=jnp.int32)
    device_ids = jnp.arange(n_req, dtype=jnp.int32)
    token_ids = jnp.arange(page_len, dtype=jnp.int32)
    spread = -(-max_pages // n_req)
    ranks = jnp.arange(spread, dtype=jnp.int32)
    match = valid[req_of] & (holder[req_of] == me)
    order = jnp.cumsum(match.astype(jnp.int32), axis=1) - 1
    picked = match[:, None, :] & (order[:, None, :] == ranks[None, :, None])
    source_slot = jnp.sum(jnp.where(picked, local_slot[req_of][:, None, :], 0), axis=-1)
    send_keys = cache_keys[source_slot]
    send_values = cache_values[source_slot]
    got_keys, got_values = (
        lax.all_to_all(send_keys, "req", split_axis=0, concat_axis=0, tiled=True),
        lax.all_to_all(send_values, "req", split_axis=0, concat_axis=0, tiled=True),
    )
    request = req_of[me]
    from_source = valid[request][None, :] & (holder[request][None, :] == device_ids[:, None])
    got_order = jnp.cumsum(from_source.astype(jnp.int32), axis=1) - 1
    got_picked = from_source[:, None, :] & (got_order[:, None, :] == ranks[None, :, None])
    page_index = jnp.sum(jnp.where(got_picked, page_ids[None, None, :], 0), axis=-1)
    present = jnp.any(got_picked, axis=-1)
    positions = page_index[..., None] * page_len + token_ids
    usable = present[..., None] & (positions < cache_lengths[request])
    flat_keys = got_keys.reshape(1, n_req * spread * page_len, heads_here, HD)
    flat_values = got_values.reshape(1, n_req * spread * page_len, heads_here, HD)
    top_d, total_d, summed_d = partial_softmax(
        own_query[None], flat_keys, flat_values, usable.reshape(1, -1), scale
    )
    top_d, total_d, summed_d = (top_d[0], total_d[0], summed_d[0])
    dec_context = finish_context(
        top_d, total_d, summed_d, own_query, own_key, own_value, scale
    ).reshape(1, cols)
    context = jnp.concatenate([pre_context, dec_context], axis=0)
    attn_terms = jnp.dot(context, w_out, preferred_element_type=jnp.float32)
    part = lax.axis_index("tensor")
    attn = lax.psum(attn_terms.astype(jnp.bfloat16), "tensor").astype(jnp.float32)
    first = norm_rows(full_rows.astype(jnp.float32) + attn, ln1_gain, ln1_bias).astype(jnp.bfloat16)
    hidden = jax.nn.gelu(
        jnp.dot(first, w_up, preferred_element_type=jnp.float32), approximate=False
    ).astype(jnp.bfloat16)
    mlp = lax.psum(
        jnp.dot(hidden, w_down, preferred_element_type=jnp.float32).astype(jnp.bfloat16), "tensor"
    ).astype(jnp.float32)
    result = norm_rows(first.astype(jnp.float32) + mlp, ln2_gain, ln2_bias).astype(jnp.bfloat16)
    result = lax.dynamic_slice_in_dim(result, part * cols, cols, 1)
    return (result[:pre_len], result[pre_len:])


def solution(mesh):
    in_specs = (
        P("req", "tensor"),
        P("req", "tensor"),
        P(),
        P(),
        P(),
        P(),
        P("req", None, "tensor"),
        P("req", None, "tensor"),
        P(None, None, "tensor"),
        P("tensor", None),
        P(),
        P(),
        P(None, "tensor"),
        P("tensor", None),
        P(),
        P(),
    )
    out_specs = (P("req", "tensor"), P("req", "tensor"))
    return jax.shard_map(local, mesh=mesh, in_specs=in_specs, out_specs=out_specs, check_vma=False)
```

profile of v0, /device:TPU:1, one launch (start us, length us, event | category | flops | bytes accessed | tf_op | source)
XLA Modules:
  0.0 413.9 jit_solution(9412859194137697735)
XLA Ops:
  7.2 0.9 copy.52
  8.2 4.5 %gather_fusion = s32[1024]{0:T(1024)S(1)} fusion(s32[576]{0:T(1024)S(1)} %copy-done.1, s32[1024]{0:T(1024)S(1)} %broadcast_clamp_fusion), kind=kCustom, calls=%fused_computation | custom fusion | bytes 12288 | tf_op jit(solution)/shard_map/gather | solution.py:111
  13.1 0.6 gather_fusion.3
  13.7 0.6 gather_fusion.1
  14.3 0.6 gather_fusion.2
  15.2 2.1 gather_fusion.4
  17.3 19.4 %all-to-all-start = ((bf16[64,1,128,128]{3,2,1,0:T(8,128)(2,1)}), bf16[64,1,128,128]{3,2,1,0:T(8,128)(2,1)S(1)}, u32[]{:S(2)}, u32[]{:S(2)}) async-start(bf16[64,1,128,128]{3,2,1,0:T(8,128)(2,1)} %bitcast.77), calls=%async_computation | async-start | bytes 4194304 | tf_op jit(solution)/shard_map/all_to_all | solution.py:126
  36.8 2.2 gather_fusion.5
  38.9 92.6 %all-to-all-done = bf16[64,1,128,128]{3,2,1,0:T(8,128)(2,1)S(1)} async-done(((bf16[64,1,128,128]{3,2,1,0:T(8,128)(2,1)}), bf16[64,1,128,128]{3,2,1,0:T(8,128)(2,1)S(1)}, u32[]{:S(2)}, u32[]{:S(2)}) %all-to-all-start) | async-done | bytes 2097184 | tf_op jit(solution)/shard_map/all_to_all | solution.py:126
  131.6 1.3 copy-done.4
  132.9 11.1 %all-to-all-start.1 = ((bf16[64,1,128,128]{3,2,1,0:T(8,128)(2,1)}), bf16[64,1,128,128]{3,2,1,0:T(8,128)(2,1)}, u32[]{:S(2)}, u32[]{:S(2)}) async-start(bf16[64,1,128,128]{3,2,1,0:T(8,128)(2,1)} %bitcast.19), calls=%async_computation.1 | async-start | bytes 4194304 | tf_op jit(solution)/shard_map/all_to_all | solution.py:127
  144.1 0.6 dynamic_slice.19
  146.0 1.4 copy.49
  147.4 13.8 %all_gather.3 = bf16[257,1024]{1,0:T(8,128)(2,1)S(1)} all-gather(bf16[257,128]{1,0:T(8,128)(2,1)S(1)} %pad_maximum_fusion), channel_id=1, replica_groups=mesh['req'=64,'tensor'=8] {'tensor'}, dimensions={1}, use_global_device_ids=true | all-gather | bytes 592128 | tf_op jit(solution)/shard_map/all_gather | solution.py:70
  164.5 0.7 fusion.68
  165.8 4.2 %copy.54 = bf16[64,1,128,128]{2,0,3,1:T(8,128)(2,1)} copy(bf16[64,1,128,128]{3,2,1,0:T(8,128)(2,1)} %copy-done.4) | data formatting | bytes 4194304 | tf_op jit(solution)/shard_map/all_to_all | solution.py:126
  169.9 4.2 %reshape.408 = bf16[8192,2,64]{0,2,1:T(8,128)(2,1)} reshape(bf16[64,1,128,128]{2,0,3,1:T(8,128)(2,1)} %copy.54) | data formatting | bytes 4194304 | tf_op jit(solution)/shard_map/reshape.19
  174.1 2.0 fusion.120
  176.8 62.2 %all-to-all-done.1 = bf16[64,1,128,128]{3,2,1,0:T(8,128)(2,1)} async-done(((bf16[64,1,128,128]{3,2,1,0:T(8,128)(2,1)}), bf16[64,1,128,128]{3,2,1,0:T(8,128)(2,1)}, u32[]{:S(2)}, u32[]{:S(2)}) %all-to-all-start.1) | async-done | bytes 2097184 | tf_op jit(solution)/shard_map/all_to_all | solution.py:127
  239.0 4.2 %copy.55 = bf16[64,1,128,128]{2,0,3,1:T(8,128)(2,1)} copy(bf16[64,1,128,128]{3,2,1,0:T(8,128)(2,1)} %all-to-all-done.1) | data formatting | bytes 4194304 | tf_op jit(solution)/shard_map/all_to_all | solution.py:127
  243.1 4.2 %reshape.409 = bf16[8192,2,64]{0,2,1:T(8,128)(2,1)} reshape(bf16[64,1,128,128]{2,0,3,1:T(8,128)(2,1)} %copy.55) | data formatting | bytes 4194304 | tf_op jit(solution)/shard_map/reshape.23
  247.3 2.3 fusion.60
  250.1 1.1 convolution_convert_fusion.1
  251.3 71.6 %all-reduce.3.cloned.1.call-done = bf16[257,1024]{1,0:T(8,128)(2,1)} async-done(((bf16[257,1024]{1,0:T(8,128)(2,1)}), bf16[257,1024]{1,0:T(8,128)(2,1)}) %all-reduce.3.cloned.1.call-update) | async-done | bytes 526352 | tf_op jit(solution)/shard_map/psum | solution.py:149
  322.9 1.3 fusion.8
  324.9 0.9 copy-done.12
  325.8 2.7 convolution_convert_fusion
  328.5 0.8 dynamic-slice.1
  329.3 0.8 dynamic-slice
  330.1 74.0 %all-reduce.5.cloned.1.call-done = bf16[257,1024]{1,0:T(8,128)(2,1)} async-done(((bf16[257,1024]{1,0:T(8,128)(2,1)}), bf16[257,1024]{1,0:T(8,128)(2,1)}) %all-reduce.5.cloned.1.call-update) | async-done | bytes 526352 | tf_op jit(solution)/shard_map/psum | solution.py:154
  404.0 1.3 fusion.10
  405.9 0.6 slice.74
  (90 shorter events, 6.8 us)
Async XLA Ops:
  7.2 317.7 %copy-start = (bf16[512,1024]{1,0:T(8,128)(2,1)S(1)}, bf16[512,1024]{1,0:T(8,128)(2,1)}, u32[]{:S(2)}) copy-start(bf16[512,1024]{1,0:T(8,128)(2,1)} %param.29) | copy-start | bytes 3145732
  7.2 1.0 copy-start.1
  8.2 4.8 %copy-start.13 = (s32[64]{0:T(128)S(1)}, s32[64]{0:T(128)}, u32[]{:S(2)}) copy-start(s32[64]{0:T(128)} %param.18) | copy-start | bytes 772
  12.7 2.5 copy-start.2
  17.3 19.4 %copy-start.3 = (bf16[9,128,128]{2,1,0:T(8,128)(2,1)S(1)}, bf16[9,128,128]{2,1,0:T(8,128)(2,1)}, u32[]{:S(2)}) copy-start(bf16[9,128,128]{2,1,0:T(8,128)(2,1)} %param.23) | copy-start | bytes 884740
  17.3 114.2 %all-to-all-start = ((bf16[64,1,128,128]{3,2,1,0:T(8,128)(2,1)}), bf16[64,1,128,128]{3,2,1,0:T(8,128)(2,1)S(1)}, u32[]{:S(2)}, u32[]{:S(2)}) async-start(bf16[64,1,128,128]{3,2,1,0:T(8,128)(2,1)} %bitcast.77), calls=%async_computation | async-start | bytes 4194304 | tf_op jit(solution)/shard_map/all_to_all | solution.py:126
  131.6 1.3 copy-start.4
  132.9 106.1 %all-to-all-start.1 = ((bf16[64,1,128,128]{3,2,1,0:T(8,128)(2,1)}), bf16[64,1,128,128]{3,2,1,0:T(8,128)(2,1)}, u32[]{:S(2)}, u32[]{:S(2)}) async-start(bf16[64,1,128,128]{3,2,1,0:T(8,128)(2,1)} %bitcast.19), calls=%async_computation.1 | async-start | bytes 4194304 | tf_op jit(solution)/shard_map/all_to_all | solution.py:127
  144.0 3.4 copy-start.8
  144.0 3.4 copy-start.11
  144.1 178.8 %all-reduce.3.cloned.1.call-start = ((), (), s32[]{:S(2)}) async-start(), calls=%async_computation.2 | async-start | bytes 1081344 | tf_op jit(solution)/shard_map/psum | solution.py:149
  161.2 1.5 copy-start.14
  247.3 2.8 copy-start.7
  251.2 73.4 %copy-start.9 = (f32[1024]{0:T(1024)S(1)}, f32[1024]{0:T(1024)}, u32[]{:S(2)}) copy-start(f32[1024]{0:T(1024)} %param.27) | copy-start | bytes 12292
  251.2 73.4 %copy-start.10 = (f32[1024]{0:T(1024)S(1)}, f32[1024]{0:T(1024)}, u32[]{:S(2)}) copy-start(f32[1024]{0:T(1024)} %param.26) | copy-start | bytes 12292
  251.2 152.8 %all-reduce.5.cloned.1.call-start = ((), (), s32[]{:S(2)}) async-start(), calls=%async_computation.3 | async-start | bytes 1081344 | tf_op jit(solution)/shard_map/psum | solution.py:154
  322.9 1.4 copy-start.5
  324.6 1.2 copy-start.12
  404.0 1.4 copy-start.6
Sparse Core Ops, SparseCore 0:
  251.3 71.4 all-reduce.2
  328.6 75.3 all-reduce.4
where the time goes:
time: 415 us; the launch traced here: 414 us
  waiting for transfers between devices  300 us (72%)
  local copies, waits for them, and re-layouts  36.9 us (9%)
  starting transfers between devices  30.6 us (7%)
  between operations  16.4 us (4%)
  blocking collectives  13.8 us (3%)
  matrix products  9.54 us (2%)
  other arithmetic  6.21 us (1%)
    all_to_all x1, waiting for transfers between devices, local(): lax.all_to_all(send_keys, 'req', split_axis=0, concat_axis=0, tiled=True)  92.6 us
    psum x1, waiting for transfers between devices, local(): lax.psum(jnp.dot(hidden, w_down, preferred_element_type=jnp.float32).asty...  74 us
    psum x1, waiting for transfers between devices, local(): lax.psum(attn_terms.astype(jnp.bfloat16), 'tensor').astype(jnp.float32)  71.6 us
    all_to_all x1, waiting for transfers between devices, local(): lax.all_to_all(send_values, 'req', split_axis=0, concat_axis=0, tiled=True)  62.2 us
    all_to_all x1, starting transfers between devices, local(): lax.all_to_all(send_keys, 'req', split_axis=0, concat_axis=0, tiled=True)  19.4 us
    all_gather x1, blocking collectives, local(): full_rows = lax.all_gather(local_rows, 'tensor', axis=1, tiled=True)  13.8 us
    all_to_all x1, starting transfers between devices, local(): lax.all_to_all(send_values, 'req', split_axis=0, concat_axis=0, tiled=True)  11.1 us
    another operation x3, local copies, waits for them, and re-layouts  8.35 us
  transfers between devices with their start and end apart: 4, of which 4 were waited for; matrix products, arithmetic and copies ran while one was open for 5% of the time, Pallas kernels for 0%

commit v1 on v0

v1 whole, which is shorter than its diff:
```python
import functools
import math

import jax
import jax.numpy as jnp
from jax import lax
from jax.experimental import pallas as pl
from jax.experimental.pallas import tpu as pltpu
from jax.sharding import PartitionSpec as P

MESH = pl.DeviceIdType.MESH
HD = 64
EPS = 1e-05
NEG = -1e30
F32 = jnp.float32
BF16 = jnp.bfloat16
TILE = 16


def dot(a, b, ca=1, cb=0):
    return lax.dot_general(a, b, (((ca,), (cb,)), ((), ())), preferred_element_type=F32)


def norm(total, gain, shift):
    mean = jnp.mean(total, axis=-1, keepdims=True)
    centered = total - mean
    var = jnp.mean(centered * centered, axis=-1, keepdims=True)
    return centered * lax.rsqrt(var + EPS) * gain + shift


def iota(shape, dim):
    return lax.broadcasted_iota(jnp.int32, shape, dim)


def kernel(
    pre_hbm, dec_hbm, req_hbm, table_hbm, place_hbm, len_hbm, keys_hbm, values_hbm,
    wqkv_hbm, wout_hbm, g1_hbm, b1_hbm, wup_hbm, wdown_hbm, g2_hbm, b2_hbm,
    pre_out, dec_out,
    x, ctx, first, wqkv, wout, wup, wdown, keys, values,
    dec_in, req, table, place, lens, g1, b1, g2, b2,
    q_all, partial, partial_all, acc, stage, from_pair, to_chip, from_chip, result, dec_term,
    local_sem, small_sem,
    x_send, x_recv, d_send, d_recv, c_send, c_recv, e_send, e_recv, w_send, w_recv,
    q_send, q_recv, p_send, p_recv, a_send, a_recv, b_send, b_recv, t_send, t_recv, o_send, o_recv,
    *, n_req, n_tensor,
):
    rows = pre_hbm.shape[0]
    cols = pre_hbm.shape[1]
    width = cols * n_tensor
    pages = keys_hbm.shape[0] // 128
    n_chip = n_tensor // 2
    share = rows // n_tensor
    me = lax.axis_index("req")
    t = lax.axis_index("tensor")
    chip = t // 2
    core = lax.rem(t, 2)
    sib = t + 1 - 2 * core

    def on_chip(k, c):
        return lax.rem(chip + k, n_chip) * 2 + c

    def send(src, dst, ss, rs, dev):
        return pltpu.make_async_remote_copy(
            src_ref=src, dst_ref=dst, send_sem=ss, recv_sem=rs, device_id=dev, device_id_type=MESH
        )

    loads = [
        (dec_hbm, dec_in), (place_hbm, place), (table_hbm, table), (req_hbm, req), (len_hbm, lens),
        (g1_hbm, g1), (b1_hbm, b1), (g2_hbm, g2), (b2_hbm, b2),
    ]
    small = [pltpu.make_async_copy(a, b, small_sem.at[i]) for i, (a, b) in enumerate(loads)]
    for copy in small:
        copy.start()

    def own_cols(ref, lo, n):
        return ref.at[pl.ds(lo, n), pl.ds(pl.multiple_of(t * cols, cols), cols)]

    def cols_of(ref, lo, n, who):
        return ref.at[pl.ds(lo, n), pl.ds(pl.multiple_of(who * cols, cols), cols)]

    big = [
        pltpu.make_async_copy(wqkv_hbm, wqkv, local_sem.at[0]),
        pltpu.make_async_copy(pre_hbm, own_cols(x, 0, rows), local_sem.at[1]),
        pltpu.make_async_copy(keys_hbm, keys, local_sem.at[2]),
        pltpu.make_async_copy(values_hbm, values, local_sem.at[3]),
        pltpu.make_async_copy(
            wout_hbm, wout.at[pl.ds(pl.multiple_of(t * cols, cols), cols), :], local_sem.at[4]
        ),
        pltpu.make_async_copy(wup_hbm, wup, local_sem.at[5]),
        pltpu.make_async_copy(wdown_hbm, wdown, local_sem.at[6]),
    ]
    for copy in big:
        copy.start()

    barrier = pltpu.get_barrier_semaphore()
    for d in range(1, n_tensor):
        pl.semaphore_signal(
            barrier, inc=1, device_id={"tensor": lax.rem(t + d, n_tensor)}, device_id_type=MESH
        )

    def greet(k, carry):
        pl.semaphore_signal(
            barrier, inc=1, device_id={"req": lax.rem(me + k, n_req)}, device_id_type=MESH
        )
        return carry

    lax.fori_loop(1, n_req, greet, 0)

    small[0].wait()
    tile = jnp.broadcast_to(dec_in[...].astype(F32), (TILE, cols)).astype(BF16)
    own_cols(x, rows, TILE)[...] = tile

    pl.semaphore_wait(barrier, n_tensor - 1 + n_req - 1)

    def tile_exchange(ref, ss, rs):
        out = []
        for d in range(1, n_tensor):
            copy = send(
                own_cols(ref, rows, TILE), own_cols(ref, rows, TILE), ss.at[d - 1], rs.at[d - 1],
                {"tensor": lax.rem(t + d, n_tensor)},
            )
            copy.start()
            out.append(copy)
        return out

    def tile_arrival(ref, ss, rs):
        for d in range(1, n_tensor):
            part = cols_of(ref, rows, TILE, lax.rem(t - d + n_tensor, n_tensor))
            send(part, part, ss.at[d - 1], rs.at[d - 1], {"tensor": sib}).wait_recv()

    def gather_start(own, region, ss, rs):
        out = []
        for k in range(1, n_chip):
            copy = send(own, region(t), ss.at[k], rs.at[k], {"tensor": on_chip(k, core)})
            copy.start()
            out.append(copy)
        copy = send(own, region(t), ss.at[0], rs.at[0], {"tensor": sib})
        copy.start()
        out.append(copy)
        return out

    def gather_forward(region, ss, rs):
        out = []
        for k in range(1, n_chip):
            part = region(on_chip(n_chip - k, core))
            send(part, part, ss.at[k], rs.at[k], {"tensor": sib}).wait_recv()
            copy = send(part, part, ss.at[n_chip - 1 + k], rs.at[n_chip - 1 + k], {"tensor": sib})
            copy.start()
            out.append(copy)
        return out

    def gather_end(region, ss, rs):
        part = region(sib)
        send(part, part, ss.at[0], rs.at[0], {"tensor": sib}).wait_recv()
        for k in range(1, n_chip):
            part = region(on_chip(n_chip - k, 1 - core))
            send(part, part, ss.at[n_chip - 1 + k], rs.at[n_chip - 1 + k], {"tensor": sib}).wait_recv()

    def x_region(who):
        return cols_of(x, 0, rows, who)

    def c_region(who):
        return cols_of(ctx, 0, rows, who)

    def w_region(who):
        return wout.at[pl.ds(pl.multiple_of(who * cols, cols), cols), :]

    pending = tile_exchange(x, d_send, d_recv)
    pending += gather_start(pre_hbm, x_region, x_send, x_recv)

    for copy in small[1:]:
        copy.wait()
    n_page_ids = place.shape[0]
    n_r = req.shape[0]
    place_row = place[...].reshape(1, n_page_ids)
    held = place_row == (iota((TILE, n_page_ids), 0) + me * pages)
    page_id = jnp.sum(
        jnp.where(held, iota((TILE, n_page_ids), 1).astype(F32), 0.0), axis=1, keepdims=True
    )
    ids = table[...].astype(F32)
    in_page = jnp.clip(
        lens[...].reshape(1, n_r) - 128 * iota(table.shape, 0), 0, 128
    ).astype(F32)
    sub = iota((TILE, n_r), 0)
    tokens = jnp.zeros((TILE, n_r), F32)
    for s in range(pages):
        hit = jnp.sum(
            jnp.where(ids == page_id[s : s + 1, 0:1], in_page, 0.0), axis=0, keepdims=True
        )
        tokens = tokens + jnp.where(sub == s, hit, 0.0)
    req_row = jnp.broadcast_to(req[...].reshape(1, n_r).astype(F32), (8, n_r))
    lane_slot = lax.rem(iota((n_r, 2 * n_r), 1), n_r)
    twice = (iota((n_r, 2 * n_r), 0) == lane_slot).astype(F32).astype(BF16)
    req_twice = dot(req_row.astype(BF16), twice)[0:1, :]
    pick = (iota((n_r, 2 * n_r), 0).astype(F32) == req_twice).astype(F32).astype(BF16)
    in_slot = dot(tokens.astype(BF16), pick)

    lane = iota((1, cols), 1)
    low_head = lane < HD
    big[0].wait()
    tile_arrival(x, d_send, d_recv)
    x_dec = x[pl.ds(rows, TILE), :]
    q_dec = dot(x_dec, wqkv[0]).astype(BF16).astype(F32)[0:1, :]
    k_dec = dot(x_dec, wqkv[1]).astype(BF16).astype(F32)[0:1, :]
    v_dec = dot(x_dec, wqkv[2]).astype(BF16).astype(F32)[0:1, :]
    q_all[pl.ds(me, 1)] = q_dec.reshape(1, 1, cols)

    def q_copy(k):
        return send(
            q_all.at[me], q_all.at[me], q_send, q_recv, {"req": lax.rem(me + k, n_req)}
        )

    def q_start(k, carry):
        q_copy(k).start()
        return carry

    lax.fori_loop(1, n_req, q_start, 0)

    pending += gather_forward(x_region, x_send, x_recv)
    pending += gather_start(wout_hbm, w_region, w_send, w_recv)
    gather_end(x_region, x_send, x_recv)
    big[1].wait()
    x_pre = x[pl.ds(0, rows), :]
    q = dot(x_pre, wqkv[0])
    k = dot(x_pre, wqkv[1]).astype(BF16)
    v = dot(x_pre, wqkv[2]).astype(BF16)
    scale = 1.0 / math.sqrt(HD)
    causal = iota((rows, rows), 0) >= iota((rows, rows), 1)
    heads = []
    for h in range(2):
        qh = jnp.where(low_head if h == 0 else ~low_head, q, 0.0).astype(BF16)
        scores = jnp.where(causal, dot(qh, k, 1, 1) * scale, NEG)
        top = jnp.max(scores, axis=-1, keepdims=True)
        weights = jnp.where(causal, jnp.exp(scores - top), 0.0)
        total = jnp.sum(weights, axis=-1, keepdims=True)
        heads.append(dot(weights.astype(BF16), v) / total)
    own_cols(ctx, 0, rows)[...] = jnp.where(low_head, heads[0], heads[1]).astype(BF16)
    pending += gather_start(own_cols(ctx, 0, rows), c_region, c_send, c_recv)

    def q_wait(ref, sem):
        pltpu.make_async_copy(ref, ref, sem).wait()

    q_wait(q_all.at[pl.ds(0, n_req - 1)], q_recv)
    q_slots = q_all[:, 0, :]
    both = jnp.concatenate(
        [jnp.where(low_head, q_slots, 0.0), jnp.where(low_head, 0.0, q_slots)], axis=0
    ).astype(BF16)
    big[2].wait()
    big[3].wait()
    scores = dot(keys[...], both, 1, 1) * scale
    row_in_page = iota((128, 2 * n_req), 0).astype(F32)
    masks = [row_in_page < in_slot[s : s + 1, :] for s in range(pages)]
    parts = [
        jnp.where(masks[s], scores[s * 128 : (s + 1) * 128], NEG) for s in range(pages)
    ]
    top = functools.reduce(jnp.maximum, parts)
    top = jnp.max(top, axis=0, keepdims=True)
    parts = [jnp.where(m, jnp.exp(p - top), 0.0) for m, p in zip(masks, parts)]
    total = jnp.sum(functools.reduce(jnp.add, parts), axis=0, keepdims=True)
    weights = jnp.concatenate(parts, axis=0).astype(BF16)
    summed = dot(weights, values[...], 0, 0)
    diag = iota((2 * n_req, 2 * n_req), 0) == iota((2 * n_req, 2 * n_req), 1)

    def per_slot(row):
        column = jnp.sum(jnp.where(diag, row, 0.0), axis=1, keepdims=True)
        return jnp.where(low_head, column[:n_req], column[n_req:])

    first_half = lax.rem(lane, HD) < HD // 2
    partial[:, 0, :] = jnp.where(low_head, summed[:n_req], summed[n_req:])
    partial[:, 1, :] = jnp.where(first_half, per_slot(top), per_slot(total))
    partial_all[pl.ds(me, 1)] = partial[pl.ds(me, 1)]

    def p_start(k, carry):
        to = lax.rem(me + k, n_req)
        send(partial.at[to], partial_all.at[me], p_send, p_recv, {"req": to}).start()
        return carry

    lax.fori_loop(1, n_req, p_start, 0)
    pending += gather_forward(c_region, c_send, c_recv)
    pending += gather_forward(w_region, w_send, w_recv)

    q_wait(partial_all.at[pl.ds(0, n_req - 1)], p_recv)
    sums = partial_all[:, 0, :]
    stats = partial_all[:, 1, :]
    tops = jnp.where(first_half, stats, pltpu.roll(stats, HD // 2, 1))
    totals = jnp.where(first_half, pltpu.roll(stats, cols - HD // 2, 1), stats)
    qk = q_dec * k_dec
    own_score = scale * jnp.where(
        low_head,
        jnp.sum(jnp.where(low_head, qk, 0.0), axis=1, keepdims=True),
        jnp.sum(jnp.where(low_head, 0.0, qk), axis=1, keepdims=True),
    )
    best = jnp.maximum(jnp.max(tops, axis=0, keepdims=True), own_score)
    factor = jnp.exp(tops - best)
    own_weight = jnp.exp(own_score - best)
    dec_total = jnp.sum(totals * factor, axis=0, keepdims=True) + own_weight
    dec_sum = jnp.sum(sums * factor, axis=0, keepdims=True) + own_weight * v_dec
    own_cols(ctx, rows, TILE)[...] = jnp.broadcast_to(dec_sum / dec_total, (TILE, cols)).astype(BF16)
    pending += tile_exchange(ctx, e_send, e_recv)

    big[4].wait()
    gather_end(w_region, w_send, w_recv)
    gather_end(c_region, c_send, c_recv)
    tile_arrival(ctx, e_send, e_recv)
    acc[...] = dot(ctx[...], wout[...])
    gain1 = g1[...].reshape(1, width)
    shift1 = b1[...].reshape(1, width)
    for lo, n in [(0, 64), (64, 64), (128, 64), (192, 64), (256, TILE)]:
        total = x[pl.ds(lo, n), :].astype(F32) + acc[pl.ds(lo, n), :]
        first[pl.ds(lo, n), :] = norm(total, gain1, shift1).astype(BF16)
    big[5].wait()
    up = dot(first[...], wup[...])
    hidden = (0.5 * up * (1.0 + lax.erf(up * (1.0 / math.sqrt(2.0))))).astype(BF16)
    big[6].wait()
    acc[...] = dot(hidden, wdown[...])
    stage[...] = acc[pl.ds(0, rows), :].astype(BF16)
    dec_term[pl.ds(t, 1)] = acc[pl.ds(rows, 1), :].astype(BF16).astype(F32).reshape(1, 1, width)

    def rows_of(who):
        return pl.ds(pl.multiple_of(who * share, share), share)

    for k in range(n_chip):
        to = on_chip(k, 1 - core)
        copy = send(stage.at[rows_of(to), :], from_pair.at[k], a_send.at[k], a_recv.at[k], {"tensor": sib})
        copy.start()
        pending.append(copy)
    for d in range(1, n_tensor):
        copy = send(
            dec_term.at[t], dec_term.at[t], t_send.at[d - 1], t_recv.at[d - 1],
            {"tensor": lax.rem(t + d, n_tensor)},
        )
        copy.start()
        pending.append(copy)
    for k in list(range(1, n_chip)) + [0]:
        to = on_chip(k, core)
        send(stage.at[rows_of(to), :], from_pair.at[k], a_send.at[k], a_recv.at[k], {"tensor": sib}).wait_recv()
        pair = stage[rows_of(to), :].astype(F32) + from_pair[k].astype(F32)
        if k:
            to_chip[k - 1] = pair.astype(BF16)
            copy = send(
                to_chip.at[k - 1], from_chip.at[k - 1], b_send.at[k - 1], b_recv.at[k - 1], {"tensor": to}
            )
            copy.start()
            pending.append(copy)

    gain2 = g2[...].reshape(1, width)
    shift2 = b2[...].reshape(1, width)
    for d in range(1, n_tensor):
        part = dec_term.at[lax.rem(t - d + n_tensor, n_tensor)]
        send(part, part, t_send.at[d - 1], t_recv.at[d - 1], {"tensor": sib}).wait_recv()
    dec_y = first[pl.ds(rows, TILE), :].astype(F32)[0:1, :] + jnp.sum(dec_term[:, 0, :], axis=0, keepdims=True)
    acc[pl.ds(rows, 8), :] = jnp.broadcast_to(norm(dec_y, gain2, shift2), (8, width))
    dec_out[...] = acc[pl.ds(rows, 8), pl.ds(pl.multiple_of(t * cols, cols), cols)][0:1, :].astype(BF16)

    y = pair + first[rows_of(t), :].astype(F32)
    for k in range(1, n_chip):
        send(
            to_chip.at[k - 1], from_chip.at[k - 1], b_send.at[k - 1], b_recv.at[k - 1], {"tensor": sib}
        ).wait_recv()
        y = y + from_chip[k - 1].astype(F32)
    result[...] = norm(y, gain2, shift2).astype(BF16)
    pre_out[rows_of(t), :] = result[:, pl.ds(pl.multiple_of(t * cols, cols), cols)]
    for d in range(1, n_tensor):
        to = lax.rem(t + d, n_tensor)
        copy = send(
            result.at[:, pl.ds(pl.multiple_of(to * cols, cols), cols)], pre_out.at[rows_of(t), :],
            o_send.at[d - 1], o_recv.at[d - 1], {"tensor": to},
        )
        copy.start()
        pending.append(copy)
    for d in range(1, n_tensor):
        part = pre_out.at[rows_of(lax.rem(t - d + n_tensor, n_tensor)), :]
        send(part, part, o_send.at[d - 1], o_recv.at[d - 1], {"tensor": sib}).wait_recv()

    q_wait(q_all.at[pl.ds(0, n_req - 1)], q_send)
    q_wait(partial.at[pl.ds(0, n_req - 1)], p_send)
    for copy in pending:
        copy.wait_send()


def local(
    pre_tokens, dec_tokens, req_of, page_table, page_place, cache_lengths, cache_keys, cache_values,
    w_qkv, w_out, ln1_gain, ln1_bias, w_up, w_down, ln2_gain, ln2_bias,
    *, n_req, n_tensor,
):
    rows, cols = pre_tokens.shape
    width = w_qkv.shape[0]
    hidden = w_up.shape[1]
    n_keys = cache_keys.shape[0] * cache_keys.shape[1]
    share = rows // n_tensor
    n_chip = n_tensor // 2
    args = (
        pre_tokens, dec_tokens, req_of, page_table.T, page_place, cache_lengths,
        cache_keys.reshape(n_keys, cols), cache_values.reshape(n_keys, cols),
        jnp.transpose(w_qkv, (1, 0, 2)), w_out, ln1_gain, ln1_bias, w_up, w_down, ln2_gain, ln2_bias,
    )
    sem = pltpu.SemaphoreType.DMA
    vm = pltpu.VMEM
    scratch = [
        vm((rows + TILE, width), BF16),
        vm((rows + TILE, width), BF16),
        vm((rows + TILE, width), BF16),
        vm((3, width, cols), BF16),
        vm((width, width), BF16),
        vm((width, hidden), BF16),
        vm((hidden, width), BF16),
        vm((n_keys, cols), BF16),
        vm((n_keys, cols), BF16),
        vm((1, cols), BF16),
        vm(req_of.shape, jnp.int32),
        vm(page_table.shape[::-1], jnp.int32),
        vm(page_place.shape, jnp.int32),
        vm(cache_lengths.shape, jnp.int32),
        vm((width,), F32), vm((width,), F32), vm((width,), F32), vm((width,), F32),
        vm((n_req, 1, cols), F32),
        vm((n_req, 2, cols), F32),
        vm((n_req, 2, cols), F32),
        vm((rows + TILE, width), F32),
        vm((rows, width), BF16),
        vm((n_chip, share, width), BF16),
        vm((n_chip - 1, share, width), BF16),
        vm((n_chip - 1, share, width), BF16),
        vm((share, width), BF16),
        vm((n_tensor, 1, width), F32),
        sem((7,)), sem((9,)),
        sem((7,)), sem((7,)), sem((7,)), sem((7,)), sem((7,)), sem((7,)), sem((7,)), sem((7,)),
        sem((7,)), sem((7,)),
        sem, sem, sem, sem,
        sem((4,)), sem((4,)), sem((3,)), sem((3,)), sem((7,)), sem((7,)), sem((7,)), sem((7,)),
    ]
    return pl.pallas_call(
        functools.partial(kernel, n_req=n_req, n_tensor=n_tensor),
        out_shape=(
            jax.ShapeDtypeStruct((rows, cols), BF16),
            jax.ShapeDtypeStruct((1, cols), BF16),
        ),
        in_specs=[pl.BlockSpec(memory_space=pltpu.HBM)] * len(args),
        out_specs=(
            pl.BlockSpec(memory_space=pltpu.VMEM),
            pl.BlockSpec(memory_space=pltpu.VMEM),
        ),
        scratch_shapes=scratch,
        compiler_params=pltpu.CompilerParams(
            collective_id=0, has_side_effects=True, vmem_limit_bytes=56 << 20
        ),
        name="layer",
    )(*args)


def solution(mesh):
    in_specs = (
        P("req", "tensor"),
        P("req", "tensor"),
        P(),
        P(),
        P(),
        P(),
        P("req", None, "tensor"),
        P("req", None, "tensor"),
        P(None, None, "tensor"),
        P("tensor", None),
        P(),
        P(),
        P(None, "tensor"),
        P("tensor", None),
        P(),
        P(),
    )
    out_specs = (P("req", "tensor"), P("req", "tensor"))
    body = functools.partial(local, n_req=mesh.shape["req"], n_tensor=mesh.shape["tensor"])
    return jax.shard_map(body, mesh=mesh, in_specs=in_specs, out_specs=out_specs, check_vma=False)
```

time: 415 us -> 62.5 us (0.15)
  waiting for transfers between devices: 300 us -> 0 us
  Pallas kernels: 0 us -> 59.7 us
  local copies, waits for them, and re-layouts: 36.9 us -> 1.99 us
  starting transfers between devices: 30.6 us -> 0 us
  between operations: 16.4 us -> 0.65 us
  blocking collectives: 13.8 us -> 0 us
  matrix products: 9.54 us -> 0 us
  other arithmetic: 6.21 us -> 0 us
    all_to_all x2 -> x0, waiting for transfers between devices: 155 us -> none  [the longest x1 92.6 us: local(): lax.all_to_all(send_keys, 'req', split_axis=0, concat_axis=0, tiled=True)]
    psum x2 -> x0, waiting for transfers between devices: 146 us -> none  [the longest x1 74 us: local(): lax.psum(jnp.dot(hidden, w_down, preferred_element_type=jnp.float32).asty...]
    pallas_call x0 -> x1, Pallas kernels: none -> 59.7 us  [local(): pl.pallas_call(functools.partial(kernel, n_req=n_req, n_tensor=n_tensor),...]
    all_to_all x2 -> x0, starting transfers between devices: 30.5 us -> none  [the longest x1 19.4 us: local(): lax.all_to_all(send_keys, 'req', split_axis=0, concat_axis=0, tiled=True)]
    all_gather x1 -> x0, blocking collectives: 13.8 us -> none  [local(): full_rows = lax.all_gather(local_rows, 'tensor', axis=1, tiled=True)]
    gather x6 -> x0, local copies, waits for them, and re-layouts: 10.6 us -> none  [the longest x1 4.53 us: local(): slots = page_place[jnp.maximum(page_table, 0)]]
    dot_general x7 -> x0, matrix products: 9.11 us -> none  [the longest x1 2.72 us: local(): jnp.dot(hidden, w_down, preferred_element_type=jnp.float32)]
    another operation x3 -> x0, local copies, waits for them, and re-layouts: 8.35 us -> none
  transfers between devices with their start and end apart: 4 -> 0, of which waited for: 4 -> 0; matrix products, arithmetic and copies ran while one was open for 5% -> 0% of each run, Pallas kernels for 0% -> 0%
where the time goes in v1:
time: 62.5 us; the launch traced here: 62.4 us
  Pallas kernels  59.7 us (96%)
  local copies, waits for them, and re-layouts  1.99 us (3%)
  between operations  0.65 us (1%)
    pallas_call x1, Pallas kernels, local(): pl.pallas_call(functools.partial(kernel, n_req=n_req, n_tensor=n_tensor),...  59.7 us
    unnamed x4, local copies, waits for them, and re-layouts  1.99 us

profile of v1, /device:TPU:1, one launch (start us, length us, event | category | flops | bytes accessed | tf_op | source)
XLA Modules:
  0.0 62.4 jit_solution(10333260658620889777)
XLA Ops:
  0.6 59.7 %layer.1 = (bf16[256,128]{1,0:T(8,128)(2,1)}, bf16[1,128]{1,0:T(2,128)(2,1)}) custom-call(bf16[256,128]{1,0:T(8,128)(2,1)} %pre_hbm.1, bf16[1,128]{1,0:T(2,128)(2,1)} %dec_hbm.1, s32[64]{0:T(128)} %req_hbm.1, s32[16,64]{1,0:T(8,128)} %bitcast.7, s32[576]{0:T(1024)} %place_hbm.1, s32[64]{0:T(128)} %len_hbm.1, bf16[1152,128]{1,0:T(8,128)(2,1)} %bitcast.5, ...), custom_call_target="tpu_custom_call" | custom-call | tf_op jit(solution)/shard_map/layer/pallas_call | solution.py:431
  60.4 0.0 copy-start
  60.4 1.5 %copy.20 = bf16[256,128]{1,0:T(8,128)(2,1)} copy(bf16[256,128]{1,0:T(8,128)(2,1)} %get-tuple-element.4) | data formatting | bytes 131072
  61.9 0.0 copy-done
  61.9 0.5 copy.21
Async XLA Ops:
  60.4 1.5 %copy-start = (bf16[1,128]{1,0:T(2,128)(2,1)S(1)}, bf16[1,128]{1,0:T(2,128)(2,1)}, u32[]{:S(2)}) copy-start(bf16[1,128]{1,0:T(2,128)(2,1)} %get-tuple-element.5) | copy-start | bytes 772

commit v2 on v1

--- a/solution.py
+++ b/solution.py
@@ -98,14 +98,21 @@
             barrier, inc=1, device_id={"tensor": lax.rem(t + d, n_tensor)}, device_id_type=MESH
         )
 
-    def greet(k, carry):
-        pl.semaphore_signal(
-            barrier, inc=1, device_id={"req": lax.rem(me + k, n_req)}, device_id_type=MESH
-        )
-        return carry
-
-    lax.fori_loop(1, n_req, greet, 0)
-
+    def each_peer(visit):
+        group = 9 if (n_req - 1) % 9 == 0 else 1
+
+        def some(i, carry):
+            for j in range(group):
+                visit(lax.rem(me + 1 + i * group + j, n_req))
+            return carry
+
+        lax.fori_loop(0, (n_req - 1) // group, some, 0)
+
+    each_peer(
+        lambda to: pl.semaphore_signal(barrier, inc=1, device_id={"req": to}, device_id_type=MESH)
+    )
+
+    pending = []
     small[0].wait()
     tile = jnp.broadcast_to(dec_in[...].astype(F32), (TILE, cols)).astype(BF16)
     own_cols(x, rows, TILE)[...] = tile
@@ -128,33 +135,32 @@
             part = cols_of(ref, rows, TILE, lax.rem(t - d + n_tensor, n_tensor))
             send(part, part, ss.at[d - 1], rs.at[d - 1], {"tensor": sib}).wait_recv()
 
-    def gather_start(own, region, ss, rs):
-        out = []
-        for k in range(1, n_chip):
-            copy = send(own, region(t), ss.at[k], rs.at[k], {"tensor": on_chip(k, core)})
+    def gather(own, region, ss, rs):
+        def go(i, src, dst, dev):
+            copy = send(src, dst, ss.at[i], rs.at[i], {"tensor": dev})
             copy.start()
-            out.append(copy)
-        copy = send(own, region(t), ss.at[0], rs.at[0], {"tensor": sib})
-        copy.start()
-        out.append(copy)
-        return out
-
-    def gather_forward(region, ss, rs):
-        out = []
-        for k in range(1, n_chip):
-            part = region(on_chip(n_chip - k, core))
-            send(part, part, ss.at[k], rs.at[k], {"tensor": sib}).wait_recv()
-            copy = send(part, part, ss.at[n_chip - 1 + k], rs.at[n_chip - 1 + k], {"tensor": sib})
-            copy.start()
-            out.append(copy)
-        return out
-
-    def gather_end(region, ss, rs):
-        part = region(sib)
-        send(part, part, ss.at[0], rs.at[0], {"tensor": sib}).wait_recv()
-        for k in range(1, n_chip):
-            part = region(on_chip(n_chip - k, 1 - core))
-            send(part, part, ss.at[n_chip - 1 + k], rs.at[n_chip - 1 + k], {"tensor": sib}).wait_recv()
+            pending.append(copy)
+
+        def arrived(i, ref):
+            send(ref, ref, ss.at[i], rs.at[i], {"tensor": sib}).wait_recv()
+
+        def begin():
+            for k in (2, 1, 3):
+                go(k, own, region(t), on_chip(k, core))
+            go(0, own, region(t), sib)
+
+        def forward():
+            for k in (1, 3, 2):
+                part = region(on_chip(n_chip - k, core))
+                arrived(k, part)
+                go(3 + k, part, part, sib)
+
+        def end():
+            arrived(0, region(sib))
+            for k in (1, 3, 2):
+                arrived(3 + k, region(on_chip(n_chip - k, 1 - core)))
+
+        return begin, forward, end
 
     def x_region(who):
         return cols_of(x, 0, rows, who)
@@ -165,9 +171,26 @@
     def w_region(who):
         return wout.at[pl.ds(pl.multiple_of(who * cols, cols), cols), :]
 
-    pending = tile_exchange(x, d_send, d_recv)
-    pending += gather_start(pre_hbm, x_region, x_send, x_recv)
-
+    gather_x = gather(pre_hbm, x_region, x_send, x_recv)
+    gather_w = gather(wout_hbm, w_region, w_send, w_recv)
+    gather_c = gather(own_cols(ctx, 0, rows), c_region, c_send, c_recv)
+
+    pending += tile_exchange(x, d_send, d_recv)
+    gather_x[0]()
+    gather_w[0]()
+
+    lane = iota((1, cols), 1)
+    low_head = lane < HD
+    big[0].wait()
+    tile_arrival(x, d_send, d_recv)
+    x_dec = x[pl.ds(rows, TILE), :]
+    q_dec = dot(x_dec, wqkv[0]).astype(BF16).astype(F32)[0:1, :]
+    q_all[pl.ds(me, 1)] = q_dec.reshape(1, 1, cols)
+    each_peer(lambda to: send(q_all.at[me], q_all.at[me], q_send, q_recv, {"req": to}).start())
+    k_dec = dot(x_dec, wqkv[1]).astype(BF16).astype(F32)[0:1, :]
+    v_dec = dot(x_dec, wqkv[2]).astype(BF16).astype(F32)[0:1, :]
+
+    gather_x[1]()
     for copy in small[1:]:
         copy.wait()
     n_page_ids = place.shape[0]
@@ -195,30 +218,7 @@
     pick = (iota((n_r, 2 * n_r), 0).astype(F32) == req_twice).astype(F32).astype(BF16)
     in_slot = dot(tokens.astype(BF16), pick)
 
-    lane = iota((1, cols), 1)
-    low_head = lane < HD
-    big[0].wait()
-    tile_arrival(x, d_send, d_recv)
-    x_dec = x[pl.ds(rows, TILE), :]
-    q_dec = dot(x_dec, wqkv[0]).astype(BF16).astype(F32)[0:1, :]
-    k_dec = dot(x_dec, wqkv[1]).astype(BF16).astype(F32)[0:1, :]
-    v_dec = dot(x_dec, wqkv[2]).astype(BF16).astype(F32)[0:1, :]
-    q_all[pl.ds(me, 1)] = q_dec.reshape(1, 1, cols)
-
-    def q_copy(k):
-        return send(
-            q_all.at[me], q_all.at[me], q_send, q_recv, {"req": lax.rem(me + k, n_req)}
-        )
-
-    def q_start(k, carry):
-        q_copy(k).start()
-        return carry
-
-    lax.fori_loop(1, n_req, q_start, 0)
-
-    pending += gather_forward(x_region, x_send, x_recv)
-    pending += gather_start(wout_hbm, w_region, w_send, w_recv)
-    gather_end(x_region, x_send, x_recv)
+    gather_x[2]()
     big[1].wait()
     x_pre = x[pl.ds(0, rows), :]
     q = dot(x_pre, wqkv[0])
@@ -235,18 +235,18 @@
         total = jnp.sum(weights, axis=-1, keepdims=True)
         heads.append(dot(weights.astype(BF16), v) / total)
     own_cols(ctx, 0, rows)[...] = jnp.where(low_head, heads[0], heads[1]).astype(BF16)
-    pending += gather_start(own_cols(ctx, 0, rows), c_region, c_send, c_recv)
+    gather_c[0]()
 
     def q_wait(ref, sem):
         pltpu.make_async_copy(ref, ref, sem).wait()
 
+    big[2].wait()
+    big[3].wait()
     q_wait(q_all.at[pl.ds(0, n_req - 1)], q_recv)
     q_slots = q_all[:, 0, :]
     both = jnp.concatenate(
         [jnp.where(low_head, q_slots, 0.0), jnp.where(low_head, 0.0, q_slots)], axis=0
     ).astype(BF16)
-    big[2].wait()
-    big[3].wait()
     scores = dot(keys[...], both, 1, 1) * scale
     row_in_page = iota((128, 2 * n_req), 0).astype(F32)
     masks = [row_in_page < in_slot[s : s + 1, :] for s in range(pages)]
@@ -269,15 +269,50 @@
     partial[:, 0, :] = jnp.where(low_head, summed[:n_req], summed[n_req:])
     partial[:, 1, :] = jnp.where(first_half, per_slot(top), per_slot(total))
     partial_all[pl.ds(me, 1)] = partial[pl.ds(me, 1)]
-
-    def p_start(k, carry):
-        to = lax.rem(me + k, n_req)
-        send(partial.at[to], partial_all.at[me], p_send, p_recv, {"req": to}).start()
-        return carry
-
-    lax.fori_loop(1, n_req, p_start, 0)
-    pending += gather_forward(c_region, c_send, c_recv)
-    pending += gather_forward(w_region, w_send, w_recv)
+    each_peer(lambda to: send(partial.at[to], partial_all.at[me], p_send, p_recv, {"req": to}).start())
+
+    gather_c[1]()
+    gather_w[1]()
+    gain1 = g1[...].reshape(1, width)
+    shift1 = b1[...].reshape(1, width)
+    gain2 = g2[...].reshape(1, width)
+    shift2 = b2[...].reshape(1, width)
+
+    def feed_forward(lo, n, chunk):
+        acc[pl.ds(lo, n), :] = dot(ctx[pl.ds(lo, n), :], wout[...])
+        for at in range(lo, lo + n, chunk):
+            total = x[pl.ds(at, chunk), :].astype(F32) + acc[pl.ds(at, chunk), :]
+            first[pl.ds(at, chunk), :] = norm(total, gain1, shift1).astype(BF16)
+        up = dot(first[pl.ds(lo, n), :], wup[...])
+        hidden = (0.5 * up * (1.0 + lax.erf(up * (1.0 / math.sqrt(2.0))))).astype(BF16)
+        return dot(hidden, wdown[...])
+
+    big[4].wait()
+    big[5].wait()
+    big[6].wait()
+    gather_c[2]()
+    gather_w[2]()
+    stage[...] = feed_forward(0, rows, 64).astype(BF16)
+
+    def rows_of(who):
+        return pl.ds(pl.multiple_of(who * share, share), share)
+
+    for k in range(n_chip):
+        to = on_chip(k, 1 - core)
+        copy = send(stage.at[rows_of(to), :], from_pair.at[k], a_send.at[k], a_recv.at[k], {"tensor": sib})
+        copy.start()
+        pending.append(copy)
+    for k in (2, 1, 3, 0):
+        to = on_chip(k, core)
+        send(stage.at[rows_of(to), :], from_pair.at[k], a_send.at[k], a_recv.at[k], {"tensor": sib}).wait_recv()
+        pair = stage[rows_of(to), :].astype(F32) + from_pair[k].astype(F32)
+        if k:
+            to_chip[k - 1] = pair.astype(BF16)
+            copy = send(
+                to_chip.at[k - 1], from_chip.at[k - 1], b_send.at[k - 1], b_recv.at[k - 1], {"tensor": to}
+            )
+            copy.start()
+            pending.append(copy)
 
     q_wait(partial_all.at[pl.ds(0, n_req - 1)], p_recv)
     sums = partial_all[:, 0, :]
@@ -298,62 +333,8 @@
     own_cols(ctx, rows, TILE)[...] = jnp.broadcast_to(dec_sum / dec_total, (TILE, cols)).astype(BF16)
     pending += tile_exchange(ctx, e_send, e_recv)
 
-    big[4].wait()
-    gather_end(w_region, w_send, w_recv)
-    gather_end(c_region, c_send, c_recv)
-    tile_arrival(ctx, e_send, e_recv)
-    acc[...] = dot(ctx[...], wout[...])
-    gain1 = g1[...].reshape(1, width)
-    shift1 = b1[...].reshape(1, width)
-    for lo, n in [(0, 64), (64, 64), (128, 64), (192, 64), (256, TILE)]:
-        total = x[pl.ds(lo, n), :].astype(F32) + acc[pl.ds(lo, n), :]
-        first[pl.ds(lo, n), :] = norm(total, gain1, shift1).astype(BF16)
-    big[5].wait()
-    up = dot(first[...], wup[...])
-    hidden = (0.5 * up * (1.0 + lax.erf(up * (1.0 / math.sqrt(2.0))))).astype(BF16)
-    big[6].wait()
-    acc[...] = dot(hidden, wdown[...])
-    stage[...] = acc[pl.ds(0, rows), :].astype(BF16)
-    dec_term[pl.ds(t, 1)] = acc[pl.ds(rows, 1), :].astype(BF16).astype(F32).reshape(1, 1, width)
-
-    def rows_of(who):
-        return pl.ds(pl.multiple_of(who * share, share), share)
-
-    for k in range(n_chip):
-        to = on_chip(k, 1 - core)
-        copy = send(stage.at[rows_of(to), :], from_pair.at[k], a_send.at[k], a_recv.at[k], {"tensor": sib})
-        copy.start()
-        pending.append(copy)
-    for d in range(1, n_tensor):
-        copy = send(
-            dec_term.at[t], dec_term.at[t], t_send.at[d - 1], t_recv.at[d - 1],
-            {"tensor": lax.rem(t + d, n_tensor)},
-        )
-        copy.start()
-        pending.append(copy)
-    for k in list(range(1, n_chip)) + [0]:
-        to = on_chip(k, core)
-        send(stage.at[rows_of(to), :], from_pair.at[k], a_send.at[k], a_recv.at[k], {"tensor": sib}).wait_recv()
-        pair = stage[rows_of(to), :].astype(F32) + from_pair[k].astype(F32)
-        if k:
-            to_chip[k - 1] = pair.astype(BF16)
-            copy = send(
-                to_chip.at[k - 1], from_chip.at[k - 1], b_send.at[k - 1], b_recv.at[k - 1], {"tensor": to}
-            )
-            copy.start()
-            pending.append(copy)
-
-    gain2 = g2[...].reshape(1, width)
-    shift2 = b2[...].reshape(1, width)
-    for d in range(1, n_tensor):
-        part = dec_term.at[lax.rem(t - d + n_tensor, n_tensor)]
-        send(part, part, t_send.at[d - 1], t_recv.at[d - 1], {"tensor": sib}).wait_recv()
-    dec_y = first[pl.ds(rows, TILE), :].astype(F32)[0:1, :] + jnp.sum(dec_term[:, 0, :], axis=0, keepdims=True)
-    acc[pl.ds(rows, 8), :] = jnp.broadcast_to(norm(dec_y, gain2, shift2), (8, width))
-    dec_out[...] = acc[pl.ds(rows, 8), pl.ds(pl.multiple_of(t * cols, cols), cols)][0:1, :].astype(BF16)
-
     y = pair + first[rows_of(t), :].astype(F32)
-    for k in range(1, n_chip):
+    for k in (1, 3, 2):
         send(
             to_chip.at[k - 1], from_chip.at[k - 1], b_send.at[k - 1], b_recv.at[k - 1], {"tensor": sib}
         ).wait_recv()
@@ -368,12 +349,29 @@
         )
         copy.start()
         pending.append(copy)
+
+    tile_arrival(ctx, e_send, e_recv)
+    term = feed_forward(rows, TILE, TILE)[0:1, :].astype(BF16).astype(F32)
+    dec_term[pl.ds(t, 1)] = term.reshape(1, 1, width)
+    for d in range(1, n_tensor):
+        copy = send(
+            dec_term.at[t], dec_term.at[t], t_send.at[d - 1], t_recv.at[d - 1],
+            {"tensor": lax.rem(t + d, n_tensor)},
+        )
+        copy.start()
+        pending.append(copy)
+    q_wait(q_all.at[pl.ds(0, n_req - 1)], q_send)
+    q_wait(partial.at[pl.ds(0, n_req - 1)], p_send)
+    for d in range(1, n_tensor):
+        part = dec_term.at[lax.rem(t - d + n_tensor, n_tensor)]
+        send(part, part, t_send.at[d - 1], t_recv.at[d - 1], {"tensor": sib}).wait_recv()
+    dec_y = first[pl.ds(rows, TILE), :].astype(F32)[0:1, :] + jnp.sum(dec_term[:, 0, :], axis=0, keepdims=True)
+    acc[pl.ds(rows, 8), :] = jnp.broadcast_to(norm(dec_y, gain2, shift2), (8, width))
+    dec_out[...] = acc[pl.ds(rows, 8), pl.ds(pl.multiple_of(t * cols, cols), cols)][0:1, :].astype(BF16)
+
     for d in range(1, n_tensor):
         part = pre_out.at[rows_of(lax.rem(t - d + n_tensor, n_tensor)), :]
         send(part, part, o_send.at[d - 1], o_recv.at[d - 1], {"tensor": sib}).wait_recv()
-
-    q_wait(q_all.at[pl.ds(0, n_req - 1)], q_send)
-    q_wait(partial.at[pl.ds(0, n_req - 1)], p_send)
     for copy in pending:
         copy.wait_send()
 
@@ -423,8 +421,8 @@
         vm((share, width), BF16),
         vm((n_tensor, 1, width), F32),
         sem((7,)), sem((9,)),
-        sem((7,)), sem((7,)), sem((7,)), sem((7,)), sem((7,)), sem((7,)), sem((7,)), sem((7,)),
-        sem((7,)), sem((7,)),
+        sem((9,)), sem((9,)), sem((7,)), sem((7,)), sem((9,)), sem((9,)), sem((7,)), sem((7,)),
+        sem((9,)), sem((9,)),
         sem, sem, sem, sem,
         sem((4,)), sem((4,)), sem((3,)), sem((3,)), sem((7,)), sem((7,)), sem((7,)), sem((7,)),
     ]

time: 62.5 us -> 59.8 us (0.957)
  Pallas kernels: 59.7 us -> 57 us
    pallas_call x1, Pallas kernels: 59.7 us -> 57 us  [local(): pl.pallas_call(functools.partial(kernel, n_req=n_req, n_tensor=n_tensor),...]
where the time goes in v2:
time: 59.8 us; the launch traced here: 59.6 us
  Pallas kernels  57 us (95%)
  local copies, waits for them, and re-layouts  1.99 us (3%)
  between operations  0.65 us (1%)
    pallas_call x1, Pallas kernels, local(): pl.pallas_call(functools.partial(kernel, n_req=n_req, n_tensor=n_tensor),...  57 us
    unnamed x4, local copies, waits for them, and re-layouts  1.99 us

profile of v2, /device:TPU:1, one launch (start us, length us, event | category | flops | bytes accessed | tf_op | source)
XLA Modules:
  0.0 59.6 jit_solution(2810943825704359771)
XLA Ops:
  0.6 57.0 %layer.1 = (bf16[256,128]{1,0:T(8,128)(2,1)}, bf16[1,128]{1,0:T(2,128)(2,1)}) custom-call(bf16[256,128]{1,0:T(8,128)(2,1)} %pre_hbm.1, bf16[1,128]{1,0:T(2,128)(2,1)} %dec_hbm.1, s32[64]{0:T(128)} %req_hbm.1, s32[16,64]{1,0:T(8,128)} %bitcast.7, s32[576]{0:T(1024)} %place_hbm.1, s32[64]{0:T(128)} %len_hbm.1, bf16[1152,128]{1,0:T(8,128)(2,1)} %bitcast.5, ...), custom_call_target="tpu_custom_call" | custom-call | tf_op jit(solution)/shard_map/layer/pallas_call | solution.py:429
  57.6 0.0 copy-start
  57.6 1.5 %copy.20 = bf16[256,128]{1,0:T(8,128)(2,1)} copy(bf16[256,128]{1,0:T(8,128)(2,1)} %get-tuple-element.4) | data formatting | bytes 131072
  59.1 0.0 copy-done
  59.1 0.5 copy.21
Async XLA Ops:
  57.6 1.5 %copy-start = (bf16[1,128]{1,0:T(2,128)(2,1)S(1)}, bf16[1,128]{1,0:T(2,128)(2,1)}, u32[]{:S(2)}) copy-start(bf16[1,128]{1,0:T(2,128)(2,1)} %get-tuple-element.5) | copy-start | bytes 772

commit v3 on v2

--- a/solution.py
+++ b/solution.py
@@ -64,6 +64,36 @@
             src_ref=src, dst_ref=dst, send_sem=ss, recv_sem=rs, device_id=dev, device_id_type=MESH
         )
 
+    n_z = 16 if n_req % 16 == 0 else n_req
+    n_y = n_req // n_z
+    ys = sorted(range(n_y), key=lambda dy: -min(dy, n_y - dy))
+
+    def each_peer(visit):
+        my, mz = me // n_z, lax.rem(me, n_z)
+
+        def visit_ring(dz, dys):
+            for dy in dys:
+                visit(lax.rem(my + dy, n_y) * n_z + lax.rem(mz + dz, n_z))
+
+        def both_ways(i, carry):
+            dz = n_z // 2 - 1 - i
+            visit_ring(dz, ys)
+            visit_ring(n_z - dz, ys)
+            return carry
+
+        visit_ring(n_z // 2, ys)
+        lax.fori_loop(0, n_z // 2 - 1, both_ways, 0)
+        visit_ring(0, [dy for dy in ys if dy])
+
+    barrier = pltpu.get_barrier_semaphore()
+    each_peer(
+        lambda to: pl.semaphore_signal(barrier, inc=1, device_id={"req": to}, device_id_type=MESH)
+    )
+    for d in range(1, n_tensor):
+        pl.semaphore_signal(
+            barrier, inc=1, device_id={"tensor": lax.rem(t + d, n_tensor)}, device_id_type=MESH
+        )
+
     loads = [
         (dec_hbm, dec_in), (place_hbm, place), (table_hbm, table), (req_hbm, req), (len_hbm, lens),
         (g1_hbm, g1), (b1_hbm, b1), (g2_hbm, g2), (b2_hbm, b2),
@@ -92,26 +122,6 @@
     for copy in big:
         copy.start()
 
-    barrier = pltpu.get_barrier_semaphore()
-    for d in range(1, n_tensor):
-        pl.semaphore_signal(
-            barrier, inc=1, device_id={"tensor": lax.rem(t + d, n_tensor)}, device_id_type=MESH
-        )
-
-    def each_peer(visit):
-        group = 9 if (n_req - 1) % 9 == 0 else 1
-
-        def some(i, carry):
-            for j in range(group):
-                visit(lax.rem(me + 1 + i * group + j, n_req))
-            return carry
-
-        lax.fori_loop(0, (n_req - 1) // group, some, 0)
-
-    each_peer(
-        lambda to: pl.semaphore_signal(barrier, inc=1, device_id={"req": to}, device_id_type=MESH)
-    )
-
     pending = []
     small[0].wait()
     tile = jnp.broadcast_to(dec_in[...].astype(F32), (TILE, cols)).astype(BF16)
@@ -121,7 +131,7 @@
 
     def tile_exchange(ref, ss, rs):
         out = []
-        for d in range(1, n_tensor):
+        for d in sorted(range(1, n_tensor), key=lambda d: abs(d - n_tensor // 2)):
             copy = send(
                 own_cols(ref, rows, TILE), own_cols(ref, rows, TILE), ss.at[d - 1], rs.at[d - 1],
                 {"tensor": lax.rem(t + d, n_tensor)},
@@ -162,6 +172,54 @@
 
         return begin, forward, end
 
+    right, left, far = on_chip(1, core), on_chip(n_chip - 1, core), on_chip(2, core)
+
+    def relay(own, region, ss, rs):
+        def halves(who):
+            ref = region(who)
+            n = ref.shape[0] // 2
+            return ref.at[pl.ds(0, n), :], ref.at[pl.ds(n, n), :]
+
+        def go(i, src, dst, dev):
+            copy = send(src, dst, ss.at[i], rs.at[i], {"tensor": dev})
+            copy.start()
+            pending.append(copy)
+
+        def arrived(i, ref):
+            send(ref, ref, ss.at[i], rs.at[i], {"tensor": sib}).wait_recv()
+
+        def begin():
+            go(1, own, region(t), right)
+            go(2, own, region(t), left)
+            go(0, own, region(t), sib)
+
+        def onward():
+            arrived(1, region(left))
+            top, _ = halves(left)
+            go(3, top, top, right)
+            arrived(2, region(right))
+            _, bottom = halves(right)
+            go(4, bottom, bottom, left)
+            go(5, region(left), region(left), sib)
+            go(6, region(right), region(right), sib)
+
+        def across():
+            top, bottom = halves(far)
+            arrived(3, top)
+            go(7, top, top, sib)
+            arrived(4, bottom)
+            go(8, bottom, bottom, sib)
+
+        def end():
+            arrived(0, region(sib))
+            arrived(5, region(on_chip(n_chip - 1, 1 - core)))
+            arrived(6, region(on_chip(1, 1 - core)))
+            top, bottom = halves(on_chip(2, 1 - core))
+            arrived(7, top)
+            arrived(8, bottom)
+
+        return begin, onward, across, end
+
     def x_region(who):
         return cols_of(x, 0, rows, who)
 
@@ -172,7 +230,7 @@
         return wout.at[pl.ds(pl.multiple_of(who * cols, cols), cols), :]
 
     gather_x = gather(pre_hbm, x_region, x_send, x_recv)
-    gather_w = gather(wout_hbm, w_region, w_send, w_recv)
+    gather_w = relay(wout_hbm, w_region, w_send, w_recv)
     gather_c = gather(own_cols(ctx, 0, rows), c_region, c_send, c_recv)
 
     pending += tile_exchange(x, d_send, d_recv)
@@ -236,6 +294,7 @@
         heads.append(dot(weights.astype(BF16), v) / total)
     own_cols(ctx, 0, rows)[...] = jnp.where(low_head, heads[0], heads[1]).astype(BF16)
     gather_c[0]()
+    gather_w[1]()
 
     def q_wait(ref, sem):
         pltpu.make_async_copy(ref, ref, sem).wait()
@@ -272,7 +331,7 @@
     each_peer(lambda to: send(partial.at[to], partial_all.at[me], p_send, p_recv, {"req": to}).start())
 
     gather_c[1]()
-    gather_w[1]()
+    gather_w[2]()
     gain1 = g1[...].reshape(1, width)
     shift1 = b1[...].reshape(1, width)
     gain2 = g2[...].reshape(1, width)
@@ -291,7 +350,7 @@
     big[5].wait()
     big[6].wait()
     gather_c[2]()
-    gather_w[2]()
+    gather_w[3]()
     stage[...] = feed_forward(0, rows, 64).astype(BF16)
 
     def rows_of(who):

time: 59.8 us -> 55.2 us (0.923)
  Pallas kernels: 57 us -> 52.4 us
    pallas_call x1, Pallas kernels: 57 us -> 52.4 us  [local(): pl.pallas_call(functools.partial(kernel, n_req=n_req, n_tensor=n_tensor),...]
where the time goes in v3:
time: 55.2 us; the launch traced here: 55 us
  Pallas kernels  52.4 us (95%)
  local copies, waits for them, and re-layouts  1.99 us (4%)
  between operations  0.65 us (1%)
    pallas_call x1, Pallas kernels, local(): pl.pallas_call(functools.partial(kernel, n_req=n_req, n_tensor=n_tensor),...  52.4 us
    unnamed x4, local copies, waits for them, and re-layouts  1.99 us

profile of v3, /device:TPU:1, one launch (start us, length us, event | category | flops | bytes accessed | tf_op | source)
XLA Modules:
  0.0 55.0 jit_solution(7083030210175851289)
XLA Ops:
  0.6 52.4 %layer.1 = (bf16[256,128]{1,0:T(8,128)(2,1)}, bf16[1,128]{1,0:T(2,128)(2,1)}) custom-call(bf16[256,128]{1,0:T(8,128)(2,1)} %pre_hbm.1, bf16[1,128]{1,0:T(2,128)(2,1)} %dec_hbm.1, s32[64]{0:T(128)} %req_hbm.1, s32[16,64]{1,0:T(8,128)} %bitcast.7, s32[576]{0:T(1024)} %place_hbm.1, s32[64]{0:T(128)} %len_hbm.1, bf16[1152,128]{1,0:T(8,128)(2,1)} %bitcast.5, ...), custom_call_target="tpu_custom_call" | custom-call | tf_op jit(solution)/shard_map/layer/pallas_call | solution.py:488
  53.0 0.0 copy-start
  53.0 1.5 %copy.20 = bf16[256,128]{1,0:T(8,128)(2,1)} copy(bf16[256,128]{1,0:T(8,128)(2,1)} %get-tuple-element.4) | data formatting | bytes 131072
  54.5 0.0 copy-done
  54.5 0.5 copy.21
Async XLA Ops:
  53.0 1.5 %copy-start = (bf16[1,128]{1,0:T(2,128)(2,1)S(1)}, bf16[1,128]{1,0:T(2,128)(2,1)}, u32[]{:S(2)}) copy-start(bf16[1,128]{1,0:T(2,128)(2,1)} %get-tuple-element.5) | copy-start | bytes 772

commit v4 on v3

--- a/solution.py
+++ b/solution.py
@@ -86,21 +86,24 @@
         visit_ring(0, [dy for dy in ys if dy])
 
     barrier = pltpu.get_barrier_semaphore()
-    each_peer(
-        lambda to: pl.semaphore_signal(barrier, inc=1, device_id={"req": to}, device_id_type=MESH)
-    )
     for d in range(1, n_tensor):
         pl.semaphore_signal(
             barrier, inc=1, device_id={"tensor": lax.rem(t + d, n_tensor)}, device_id_type=MESH
         )
+    each_peer(
+        lambda to: pl.semaphore_signal(barrier, inc=1, device_id={"req": to}, device_id_type=MESH)
+    )
 
     loads = [
         (dec_hbm, dec_in), (place_hbm, place), (table_hbm, table), (req_hbm, req), (len_hbm, lens),
         (g1_hbm, g1), (b1_hbm, b1), (g2_hbm, g2), (b2_hbm, b2),
     ]
     small = [pltpu.make_async_copy(a, b, small_sem.at[i]) for i, (a, b) in enumerate(loads)]
-    for copy in small:
-        copy.start()
+    small[0].start()
+
+    def start_loads():
+        for copy in big + small[1:]:
+            copy.start()
 
     def own_cols(ref, lo, n):
         return ref.at[pl.ds(lo, n), pl.ds(pl.multiple_of(t * cols, cols), cols)]
@@ -119,8 +122,6 @@
         pltpu.make_async_copy(wup_hbm, wup, local_sem.at[5]),
         pltpu.make_async_copy(wdown_hbm, wdown, local_sem.at[6]),
     ]
-    for copy in big:
-        copy.start()
 
     pending = []
     small[0].wait()
@@ -159,8 +160,8 @@
                 go(k, own, region(t), on_chip(k, core))
             go(0, own, region(t), sib)
 
-        def forward():
-            for k in (1, 3, 2):
+        def forward(*ks):
+            for k in ks:
                 part = region(on_chip(n_chip - k, core))
                 arrived(k, part)
                 go(3 + k, part, part, sib)
@@ -175,8 +176,7 @@
     right, left, far = on_chip(1, core), on_chip(n_chip - 1, core), on_chip(2, core)
 
     def relay(own, region, ss, rs):
-        def halves(who):
-            ref = region(who)
+        def split(ref):
             n = ref.shape[0] // 2
             return ref.at[pl.ds(0, n), :], ref.at[pl.ds(n, n), :]
 
@@ -189,36 +189,42 @@
             send(ref, ref, ss.at[i], rs.at[i], {"tensor": sib}).wait_recv()
 
         def begin():
-            go(1, own, region(t), right)
-            go(2, own, region(t), left)
+            (own_top, own_bottom), (top, bottom) = split(own), split(region(t))
+            go(1, own_top, top, right)
+            go(2, own_bottom, bottom, left)
+            go(3, own_bottom, bottom, right)
+            go(4, own_top, top, left)
             go(0, own, region(t), sib)
 
         def onward():
-            arrived(1, region(left))
-            top, _ = halves(left)
-            go(3, top, top, right)
-            arrived(2, region(right))
-            _, bottom = halves(right)
-            go(4, bottom, bottom, left)
-            go(5, region(left), region(left), sib)
-            go(6, region(right), region(right), sib)
+            top, _ = split(region(left))
+            arrived(1, top)
+            go(5, top, top, right)
+            _, bottom = split(region(right))
+            arrived(2, bottom)
+            go(6, bottom, bottom, left)
+
+        def near():
+            _, bottom = split(region(left))
+            arrived(3, bottom)
+            go(7, region(left), region(left), sib)
+            top, _ = split(region(right))
+            arrived(4, top)
+            go(8, region(right), region(right), sib)
 
         def across():
-            top, bottom = halves(far)
-            arrived(3, top)
-            go(7, top, top, sib)
-            arrived(4, bottom)
-            go(8, bottom, bottom, sib)
+            top, bottom = split(region(far))
+            arrived(5, top)
+            arrived(6, bottom)
+            go(9, region(far), region(far), sib)
 
         def end():
             arrived(0, region(sib))
-            arrived(5, region(on_chip(n_chip - 1, 1 - core)))
-            arrived(6, region(on_chip(1, 1 - core)))
-            top, bottom = halves(on_chip(2, 1 - core))
-            arrived(7, top)
-            arrived(8, bottom)
-
-        return begin, onward, across, end
+            arrived(7, region(on_chip(n_chip - 1, 1 - core)))
+            arrived(8, region(on_chip(1, 1 - core)))
+            arrived(9, region(on_chip(2, 1 - core)))
+
+        return begin, onward, near, across, end
 
     def x_region(who):
         return cols_of(x, 0, rows, who)
@@ -235,6 +241,7 @@
 
     pending += tile_exchange(x, d_send, d_recv)
     gather_x[0]()
+    start_loads()
     gather_w[0]()
 
     lane = iota((1, cols), 1)
@@ -248,7 +255,7 @@
     k_dec = dot(x_dec, wqkv[1]).astype(BF16).astype(F32)[0:1, :]
     v_dec = dot(x_dec, wqkv[2]).astype(BF16).astype(F32)[0:1, :]
 
-    gather_x[1]()
+    gather_x[1](1, 3, 2)
     for copy in small[1:]:
         copy.wait()
     n_page_ids = place.shape[0]
@@ -276,6 +283,7 @@
     pick = (iota((n_r, 2 * n_r), 0).astype(F32) == req_twice).astype(F32).astype(BF16)
     in_slot = dot(tokens.astype(BF16), pick)
 
+    gather_w[1]()
     gather_x[2]()
     big[1].wait()
     x_pre = x[pl.ds(0, rows), :]
@@ -294,7 +302,6 @@
         heads.append(dot(weights.astype(BF16), v) / total)
     own_cols(ctx, 0, rows)[...] = jnp.where(low_head, heads[0], heads[1]).astype(BF16)
     gather_c[0]()
-    gather_w[1]()
 
     def q_wait(ref, sem):
         pltpu.make_async_copy(ref, ref, sem).wait()
@@ -330,8 +337,9 @@
     partial_all[pl.ds(me, 1)] = partial[pl.ds(me, 1)]
     each_peer(lambda to: send(partial.at[to], partial_all.at[me], p_send, p_recv, {"req": to}).start())
 
-    gather_c[1]()
     gather_w[2]()
+    gather_c[1](1, 3, 2)
+    gather_w[3]()
     gain1 = g1[...].reshape(1, width)
     shift1 = b1[...].reshape(1, width)
     gain2 = g2[...].reshape(1, width)
@@ -346,11 +354,51 @@
         hidden = (0.5 * up * (1.0 + lax.erf(up * (1.0 / math.sqrt(2.0))))).astype(BF16)
         return dot(hidden, wdown[...])
 
+    def dec_merge():
+        q_wait(partial_all.at[pl.ds(0, n_req - 1)], p_recv)
+        sums = partial_all[:, 0, :]
+        stats = partial_all[:, 1, :]
+        tops = jnp.where(first_half, stats, pltpu.roll(stats, HD // 2, 1))
+        totals = jnp.where(first_half, pltpu.roll(stats, cols - HD // 2, 1), stats)
+        qk = q_dec * k_dec
+        own_score = scale * jnp.where(
+            low_head,
+            jnp.sum(jnp.where(low_head, qk, 0.0), axis=1, keepdims=True),
+            jnp.sum(jnp.where(low_head, 0.0, qk), axis=1, keepdims=True),
+        )
+        best = jnp.maximum(jnp.max(tops, axis=0, keepdims=True), own_score)
+        factor = jnp.exp(tops - best)
+        own_weight = jnp.exp(own_score - best)
+        dec_total = jnp.sum(totals * factor, axis=0, keepdims=True) + own_weight
+        dec_sum = jnp.sum(sums * factor, axis=0, keepdims=True) + own_weight * v_dec
+        own_cols(ctx, rows, TILE)[...] = jnp.broadcast_to(dec_sum / dec_total, (TILE, cols)).astype(BF16)
+        pending.extend(tile_exchange(ctx, e_send, e_recv))
+
+    last = []
+
+    def dec_tail():
+        tile_arrival(ctx, e_send, e_recv)
+        term = feed_forward(rows, TILE, TILE)[0:1, :].astype(BF16).astype(F32)
+        dec_term[pl.ds(t, 1)] = term.reshape(1, 1, width)
+        for d in range(1, n_tensor):
+            copy = send(
+                dec_term.at[t], dec_term.at[t], t_send.at[d - 1], t_recv.at[d - 1],
+                {"tensor": lax.rem(t + d, n_tensor)},
+            )
+            copy.start()
+            last.append(copy)
+
+    def drain():
+        q_wait(q_all.at[pl.ds(0, n_req - 1)], q_send)
+        q_wait(partial.at[pl.ds(0, n_req - 1)], p_send)
+        for copy in pending:
+            copy.wait_send()
+
     big[4].wait()
     big[5].wait()
     big[6].wait()
     gather_c[2]()
-    gather_w[3]()
+    gather_w[4]()
     stage[...] = feed_forward(0, rows, 64).astype(BF16)
 
     def rows_of(who):
@@ -361,6 +409,7 @@
         copy = send(stage.at[rows_of(to), :], from_pair.at[k], a_send.at[k], a_recv.at[k], {"tensor": sib})
         copy.start()
         pending.append(copy)
+    dec_merge()
     for k in (2, 1, 3, 0):
         to = on_chip(k, core)
         send(stage.at[rows_of(to), :], from_pair.at[k], a_send.at[k], a_recv.at[k], {"tensor": sib}).wait_recv()
@@ -373,24 +422,7 @@
             copy.start()
             pending.append(copy)
 
-    q_wait(partial_all.at[pl.ds(0, n_req - 1)], p_recv)
-    sums = partial_all[:, 0, :]
-    stats = partial_all[:, 1, :]
-    tops = jnp.where(first_half, stats, pltpu.roll(stats, HD // 2, 1))
-    totals = jnp.where(first_half, pltpu.roll(stats, cols - HD // 2, 1), stats)
-    qk = q_dec * k_dec
-    own_score = scale * jnp.where(
-        low_head,
-        jnp.sum(jnp.where(low_head, qk, 0.0), axis=1, keepdims=True),
-        jnp.sum(jnp.where(low_head, 0.0, qk), axis=1, keepdims=True),
-    )
-    best = jnp.maximum(jnp.max(tops, axis=0, keepdims=True), own_score)
-    factor = jnp.exp(tops - best)
-    own_weight = jnp.exp(own_score - best)
-    dec_total = jnp.sum(totals * factor, axis=0, keepdims=True) + own_weight
-    dec_sum = jnp.sum(sums * factor, axis=0, keepdims=True) + own_weight * v_dec
-    own_cols(ctx, rows, TILE)[...] = jnp.broadcast_to(dec_sum / dec_total, (TILE, cols)).astype(BF16)
-    pending += tile_exchange(ctx, e_send, e_recv)
+    dec_tail()
 
     y = pair + first[rows_of(t), :].astype(F32)
     for k in (1, 3, 2):
@@ -409,18 +441,8 @@
         copy.start()
         pending.append(copy)
 
-    tile_arrival(ctx, e_send, e_recv)
-    term = feed_forward(rows, TILE, TILE)[0:1, :].astype(BF16).astype(F32)
-    dec_term[pl.ds(t, 1)] = term.reshape(1, 1, width)
-    for d in range(1, n_tensor):
-        copy = send(
-            dec_term.at[t], dec_term.at[t], t_send.at[d - 1], t_recv.at[d - 1],
-            {"tensor": lax.rem(t + d, n_tensor)},
-        )
-        copy.start()
-        pending.append(copy)
-    q_wait(q_all.at[pl.ds(0, n_req - 1)], q_send)
-    q_wait(partial.at[pl.ds(0, n_req - 1)], p_send)
+    drain()
+
     for d in range(1, n_tensor):
         part = dec_term.at[lax.rem(t - d + n_tensor, n_tensor)]
         send(part, part, t_send.at[d - 1], t_recv.at[d - 1], {"tensor": sib}).wait_recv()
@@ -431,7 +453,7 @@
     for d in range(1, n_tensor):
         part = pre_out.at[rows_of(lax.rem(t - d + n_tensor, n_tensor)), :]
         send(part, part, o_send.at[d - 1], o_recv.at[d - 1], {"tensor": sib}).wait_recv()
-    for copy in pending:
+    for copy in last:
         copy.wait_send()
 
 
@@ -481,7 +503,7 @@
         vm((n_tensor, 1, width), F32),
         sem((7,)), sem((9,)),
         sem((9,)), sem((9,)), sem((7,)), sem((7,)), sem((9,)), sem((9,)), sem((7,)), sem((7,)),
-        sem((9,)), sem((9,)),
+        sem((10,)), sem((10,)),
         sem, sem, sem, sem,
         sem((4,)), sem((4,)), sem((3,)), sem((3,)), sem((7,)), sem((7,)), sem((7,)), sem((7,)),
     ]

time: 55.2 us -> 53.5 us (0.969)
  Pallas kernels: 52.4 us -> 50.6 us
    pallas_call x1, Pallas kernels: 52.4 us -> 50.6 us  [local(): pl.pallas_call(functools.partial(kernel, n_req=n_req, n_tensor=n_tensor),...]
where the time goes in v4:
time: 53.5 us; the launch traced here: 53.3 us
  Pallas kernels  50.6 us (95%)
  local copies, waits for them, and re-layouts  1.99 us (4%)
  between operations  0.65 us (1%)
    pallas_call x1, Pallas kernels, local(): pl.pallas_call(functools.partial(kernel, n_req=n_req, n_tensor=n_tensor),...  50.6 us
    unnamed x4, local copies, waits for them, and re-layouts  1.99 us

profile of v4, /device:TPU:1, one launch (start us, length us, event | category | flops | bytes accessed | tf_op | source)
XLA Modules:
  0.0 53.3 jit_solution(1775588835262432283)
XLA Ops:
  0.6 50.6 %layer.1 = (bf16[256,128]{1,0:T(8,128)(2,1)}, bf16[1,128]{1,0:T(2,128)(2,1)}) custom-call(bf16[256,128]{1,0:T(8,128)(2,1)} %pre_hbm.1, bf16[1,128]{1,0:T(2,128)(2,1)} %dec_hbm.1, s32[64]{0:T(128)} %req_hbm.1, s32[16,64]{1,0:T(8,128)} %bitcast.7, s32[576]{0:T(1024)} %place_hbm.1, s32[64]{0:T(128)} %len_hbm.1, bf16[1152,128]{1,0:T(8,128)(2,1)} %bitcast.5, ...), custom_call_target="tpu_custom_call" | custom-call | tf_op jit(solution)/shard_map/layer/pallas_call | solution.py:510
  51.3 0.0 copy-start
  51.3 1.5 %copy.20 = bf16[256,128]{1,0:T(8,128)(2,1)} copy(bf16[256,128]{1,0:T(8,128)(2,1)} %get-tuple-element.4) | data formatting | bytes 131072
  52.8 0.0 copy-done
  52.8 0.5 copy.21
Async XLA Ops:
  51.3 1.5 %copy-start = (bf16[1,128]{1,0:T(2,128)(2,1)S(1)}, bf16[1,128]{1,0:T(2,128)(2,1)}, u32[]{:S(2)}) copy-start(bf16[1,128]{1,0:T(2,128)(2,1)} %get-tuple-element.5) | copy-start | bytes 772

commit v5 on v4

--- a/solution.py
+++ b/solution.py
@@ -39,7 +39,7 @@
     x, ctx, first, wqkv, wout, wup, wdown, keys, values,
     dec_in, req, table, place, lens, g1, b1, g2, b2,
     q_all, partial, partial_all, acc, stage, from_pair, to_chip, from_chip, result, dec_term,
-    local_sem, small_sem,
+    local_sem, small_sem, ring_in,
     x_send, x_recv, d_send, d_recv, c_send, c_recv, e_send, e_recv, w_send, w_recv,
     q_send, q_recv, p_send, p_recv, a_send, a_recv, b_send, b_recv, t_send, t_recv, o_send, o_recv,
     *, n_req, n_tensor,
@@ -90,9 +90,14 @@
         pl.semaphore_signal(
             barrier, inc=1, device_id={"tensor": lax.rem(t + d, n_tensor)}, device_id_type=MESH
         )
-    each_peer(
-        lambda to: pl.semaphore_signal(barrier, inc=1, device_id={"req": to}, device_id_type=MESH)
-    )
+    my, mz = me // n_z, lax.rem(me, n_z)
+    columns = [lax.rem(my + dy, n_y) * n_z + mz for dy in ys if dy]
+    ring = [
+        my * n_z + lax.rem(mz + dz, n_z)
+        for dz in sorted(range(1, n_z), key=lambda dz: -min(dz, n_z - dz))
+    ]
+    for to in ring + columns:
+        pl.semaphore_signal(barrier, inc=1, device_id={"req": to}, device_id_type=MESH)
 
     loads = [
         (dec_hbm, dec_in), (place_hbm, place), (table_hbm, table), (req_hbm, req), (len_hbm, lens),
@@ -128,7 +133,9 @@
     tile = jnp.broadcast_to(dec_in[...].astype(F32), (TILE, cols)).astype(BF16)
     own_cols(x, rows, TILE)[...] = tile
 
-    pl.semaphore_wait(barrier, n_tensor - 1 + n_req - 1)
+    pl.semaphore_wait(barrier, n_tensor - 1 + len(ring) + len(columns))
+    for to in columns:
+        pl.semaphore_signal(ring_in, inc=1, device_id={"req": to}, device_id_type=MESH)
 
     def tile_exchange(ref, ss, rs):
         out = []
@@ -251,6 +258,7 @@
     x_dec = x[pl.ds(rows, TILE), :]
     q_dec = dot(x_dec, wqkv[0]).astype(BF16).astype(F32)[0:1, :]
     q_all[pl.ds(me, 1)] = q_dec.reshape(1, 1, cols)
+    pl.semaphore_wait(ring_in, len(columns))
     each_peer(lambda to: send(q_all.at[me], q_all.at[me], q_send, q_recv, {"req": to}).start())
     k_dec = dot(x_dec, wqkv[1]).astype(BF16).astype(F32)[0:1, :]
     v_dec = dot(x_dec, wqkv[2]).astype(BF16).astype(F32)[0:1, :]
@@ -501,7 +509,7 @@
         vm((n_chip - 1, share, width), BF16),
         vm((share, width), BF16),
         vm((n_tensor, 1, width), F32),
-        sem((7,)), sem((9,)),
+        sem((9,)), sem((9,)), pltpu.SemaphoreType.REGULAR,
         sem((9,)), sem((9,)), sem((7,)), sem((7,)), sem((9,)), sem((9,)), sem((7,)), sem((7,)),
         sem((10,)), sem((10,)),
         sem, sem, sem, sem,

time: 53.5 us -> 51.9 us (0.970)
  Pallas kernels: 50.6 us -> 49.1 us
    pallas_call x1, Pallas kernels: 50.6 us -> 49.1 us  [local(): pl.pallas_call(functools.partial(kernel, n_req=n_req, n_tensor=n_tensor),...]
where the time goes in v5:
time: 51.9 us; the launch traced here: 51.7 us
  Pallas kernels  49.1 us (95%)
  local copies, waits for them, and re-layouts  1.99 us (4%)
  between operations  0.65 us (1%)
    pallas_call x1, Pallas kernels, local(): pl.pallas_call(functools.partial(kernel, n_req=n_req, n_tensor=n_tensor),...  49.1 us
    unnamed x4, local copies, waits for them, and re-layouts  1.99 us

profile of v5, /device:TPU:1, one launch (start us, length us, event | category | flops | bytes accessed | tf_op | source)
XLA Modules:
  0.0 51.7 jit_solution(1804159946182446227)
XLA Ops:
  0.6 49.1 %layer.1 = (bf16[256,128]{1,0:T(8,128)(2,1)}, bf16[1,128]{1,0:T(2,128)(2,1)}) custom-call(bf16[256,128]{1,0:T(8,128)(2,1)} %pre_hbm.1, bf16[1,128]{1,0:T(2,128)(2,1)} %dec_hbm.1, s32[64]{0:T(128)} %req_hbm.1, s32[16,64]{1,0:T(8,128)} %bitcast.7, s32[576]{0:T(1024)} %place_hbm.1, s32[64]{0:T(128)} %len_hbm.1, bf16[1152,128]{1,0:T(8,128)(2,1)} %bitcast.5, ...), custom_call_target="tpu_custom_call" | custom-call | tf_op jit(solution)/shard_map/layer/pallas_call | solution.py:518
  49.7 0.0 copy-start
  49.7 1.5 %copy.20 = bf16[256,128]{1,0:T(8,128)(2,1)} copy(bf16[256,128]{1,0:T(8,128)(2,1)} %get-tuple-element.4) | data formatting | bytes 131072
  51.2 0.0 copy-done
  51.2 0.5 copy.21
Async XLA Ops:
  49.7 1.5 %copy-start = (bf16[1,128]{1,0:T(2,128)(2,1)S(1)}, bf16[1,128]{1,0:T(2,128)(2,1)}, u32[]{:S(2)}) copy-start(bf16[1,128]{1,0:T(2,128)(2,1)} %get-tuple-element.5) | copy-start | bytes 772

commit v6 on v5

--- a/solution.py
+++ b/solution.py
@@ -39,7 +39,7 @@
     x, ctx, first, wqkv, wout, wup, wdown, keys, values,
     dec_in, req, table, place, lens, g1, b1, g2, b2,
     q_all, partial, partial_all, acc, stage, from_pair, to_chip, from_chip, result, dec_term,
-    local_sem, small_sem, ring_in,
+    local_sem, small_sem, near_in, ring_in,
     x_send, x_recv, d_send, d_recv, c_send, c_recv, e_send, e_recv, w_send, w_recv,
     q_send, q_recv, p_send, p_recv, a_send, a_recv, b_send, b_recv, t_send, t_recv, o_send, o_recv,
     *, n_req, n_tensor,
@@ -92,11 +92,13 @@
         )
     my, mz = me // n_z, lax.rem(me, n_z)
     columns = [lax.rem(my + dy, n_y) * n_z + mz for dy in ys if dy]
-    ring = [
+    reach = n_z // 4
+    near = [
         my * n_z + lax.rem(mz + dz, n_z)
-        for dz in sorted(range(1, n_z), key=lambda dz: -min(dz, n_z - dz))
+        for d in range(reach, 0, -1)
+        for dz in (d, n_z - d)
     ]
-    for to in ring + columns:
+    for to in near + columns:
         pl.semaphore_signal(barrier, inc=1, device_id={"req": to}, device_id_type=MESH)
 
     loads = [
@@ -133,9 +135,9 @@
     tile = jnp.broadcast_to(dec_in[...].astype(F32), (TILE, cols)).astype(BF16)
     own_cols(x, rows, TILE)[...] = tile
 
-    pl.semaphore_wait(barrier, n_tensor - 1 + len(ring) + len(columns))
-    for to in columns:
-        pl.semaphore_signal(ring_in, inc=1, device_id={"req": to}, device_id_type=MESH)
+    pl.semaphore_wait(barrier, n_tensor - 1 + len(near) + len(columns))
+    for to in near[:2]:
+        pl.semaphore_signal(near_in, inc=1, device_id={"req": to}, device_id_type=MESH)
 
     def tile_exchange(ref, ss, rs):
         out = []
@@ -248,22 +250,12 @@
 
     pending += tile_exchange(x, d_send, d_recv)
     gather_x[0]()
+    gather_w[0]()
     start_loads()
-    gather_w[0]()
-
-    lane = iota((1, cols), 1)
-    low_head = lane < HD
-    big[0].wait()
-    tile_arrival(x, d_send, d_recv)
-    x_dec = x[pl.ds(rows, TILE), :]
-    q_dec = dot(x_dec, wqkv[0]).astype(BF16).astype(F32)[0:1, :]
-    q_all[pl.ds(me, 1)] = q_dec.reshape(1, 1, cols)
-    pl.semaphore_wait(ring_in, len(columns))
-    each_peer(lambda to: send(q_all.at[me], q_all.at[me], q_send, q_recv, {"req": to}).start())
-    k_dec = dot(x_dec, wqkv[1]).astype(BF16).astype(F32)[0:1, :]
-    v_dec = dot(x_dec, wqkv[2]).astype(BF16).astype(F32)[0:1, :]
-
-    gather_x[1](1, 3, 2)
+    pl.semaphore_wait(near_in, 2)
+    for to in columns:
+        pl.semaphore_signal(ring_in, inc=1, device_id={"req": to}, device_id_type=MESH)
+
     for copy in small[1:]:
         copy.wait()
     n_page_ids = place.shape[0]
@@ -291,6 +283,19 @@
     pick = (iota((n_r, 2 * n_r), 0).astype(F32) == req_twice).astype(F32).astype(BF16)
     in_slot = dot(tokens.astype(BF16), pick)
 
+    lane = iota((1, cols), 1)
+    low_head = lane < HD
+    big[0].wait()
+    tile_arrival(x, d_send, d_recv)
+    x_dec = x[pl.ds(rows, TILE), :]
+    q_dec = dot(x_dec, wqkv[0]).astype(BF16).astype(F32)[0:1, :]
+    q_all[pl.ds(me, 1)] = q_dec.reshape(1, 1, cols)
+    pl.semaphore_wait(ring_in, len(columns))
+    each_peer(lambda to: send(q_all.at[me], q_all.at[me], q_send, q_recv, {"req": to}).start())
+    k_dec = dot(x_dec, wqkv[1]).astype(BF16).astype(F32)[0:1, :]
+    v_dec = dot(x_dec, wqkv[2]).astype(BF16).astype(F32)[0:1, :]
+
+    gather_x[1](1, 3, 2)
     gather_w[1]()
     gather_x[2]()
     big[1].wait()
@@ -509,7 +514,7 @@
         vm((n_chip - 1, share, width), BF16),
         vm((share, width), BF16),
         vm((n_tensor, 1, width), F32),
-        sem((9,)), sem((9,)), pltpu.SemaphoreType.REGULAR,
+        sem((9,)), sem((9,)), pltpu.SemaphoreType.REGULAR, pltpu.SemaphoreType.REGULAR,
         sem((9,)), sem((9,)), sem((7,)), sem((7,)), sem((9,)), sem((9,)), sem((7,)), sem((7,)),
         sem((10,)), sem((10,)),
         sem, sem, sem, sem,

time: 51.9 us -> 50.7 us (0.977)
  Pallas kernels: 49.1 us -> 47.9 us
    pallas_call x1, Pallas kernels: 49.1 us -> 47.9 us  [local(): pl.pallas_call(functools.partial(kernel, n_req=n_req, n_tensor=n_tensor),...]
where the time goes in v6:
time: 50.7 us; the launch traced here: 50.6 us
  Pallas kernels  47.9 us (94%)
  local copies, waits for them, and re-layouts  1.99 us (4%)
  between operations  0.65 us (1%)
    pallas_call x1, Pallas kernels, local(): pl.pallas_call(functools.partial(kernel, n_req=n_req, n_tensor=n_tensor),...  47.9 us
    unnamed x4, local copies, waits for them, and re-layouts  1.99 us

profile of v6, /device:TPU:1, one launch (start us, length us, event | category | flops | bytes accessed | tf_op | source)
XLA Modules:
  0.0 50.6 jit_solution(16920905888290218074)
XLA Ops:
  0.6 47.9 %layer.1 = (bf16[256,128]{1,0:T(8,128)(2,1)}, bf16[1,128]{1,0:T(2,128)(2,1)}) custom-call(bf16[256,128]{1,0:T(8,128)(2,1)} %pre_hbm.1, bf16[1,128]{1,0:T(2,128)(2,1)} %dec_hbm.1, s32[64]{0:T(128)} %req_hbm.1, s32[16,64]{1,0:T(8,128)} %bitcast.7, s32[576]{0:T(1024)} %place_hbm.1, s32[64]{0:T(128)} %len_hbm.1, bf16[1152,128]{1,0:T(8,128)(2,1)} %bitcast.5, ...), custom_call_target="tpu_custom_call" | custom-call | tf_op jit(solution)/shard_map/layer/pallas_call | solution.py:523
  48.6 0.0 copy-start
  48.6 1.5 %copy.20 = bf16[256,128]{1,0:T(8,128)(2,1)} copy(bf16[256,128]{1,0:T(8,128)(2,1)} %get-tuple-element.4) | data formatting | bytes 131072
  50.0 0.0 copy-done
  50.0 0.5 %copy.21 = bf16[1,128]{1,0:T(2,128)(2,1)} copy(bf16[1,128]{1,0:T(2,128)(2,1)S(1)} %copy-done) | data formatting | bytes 512
Async XLA Ops:
  48.6 1.5 %copy-start = (bf16[1,128]{1,0:T(2,128)(2,1)S(1)}, bf16[1,128]{1,0:T(2,128)(2,1)}, u32[]{:S(2)}) copy-start(bf16[1,128]{1,0:T(2,128)(2,1)} %get-tuple-element.5) | copy-start | bytes 772

commit v7 on v6

--- a/solution.py
+++ b/solution.py
@@ -422,7 +422,6 @@
         copy = send(stage.at[rows_of(to), :], from_pair.at[k], a_send.at[k], a_recv.at[k], {"tensor": sib})
         copy.start()
         pending.append(copy)
-    dec_merge()
     for k in (2, 1, 3, 0):
         to = on_chip(k, core)
         send(stage.at[rows_of(to), :], from_pair.at[k], a_send.at[k], a_recv.at[k], {"tensor": sib}).wait_recv()
@@ -435,6 +434,7 @@
             copy.start()
             pending.append(copy)
 
+    dec_merge()
     dec_tail()
 
     y = pair + first[rows_of(t), :].astype(F32)

time: 50.7 us -> 50.3 us (level)
  no operation moved by 1% of the time
where the time goes in v7:
time: 50.3 us; the launch traced here: 50.2 us
  Pallas kernels  47.5 us (94%)
  local copies, waits for them, and re-layouts  1.99 us (4%)
  between operations  0.65 us (1%)
    pallas_call x1, Pallas kernels, local(): pl.pallas_call(functools.partial(kernel, n_req=n_req, n_tensor=n_tensor),...  47.5 us
    unnamed x4, local copies, waits for them, and re-layouts  1.99 us

profile of v7, /device:TPU:1, one launch (start us, length us, event | category | flops | bytes accessed | tf_op | source)
XLA Modules:
  0.0 50.2 jit_solution(1554577012997410516)
XLA Ops:
  0.6 47.5 %layer.1 = (bf16[256,128]{1,0:T(8,128)(2,1)}, bf16[1,128]{1,0:T(2,128)(2,1)}) custom-call(bf16[256,128]{1,0:T(8,128)(2,1)} %pre_hbm.1, bf16[1,128]{1,0:T(2,128)(2,1)} %dec_hbm.1, s32[64]{0:T(128)} %req_hbm.1, s32[16,64]{1,0:T(8,128)} %bitcast.7, s32[576]{0:T(1024)} %place_hbm.1, s32[64]{0:T(128)} %len_hbm.1, bf16[1152,128]{1,0:T(8,128)(2,1)} %bitcast.5, ...), custom_call_target="tpu_custom_call" | custom-call | tf_op jit(solution)/shard_map/layer/pallas_call | solution.py:523
  48.2 0.0 copy-start
  48.2 1.5 %copy.20 = bf16[256,128]{1,0:T(8,128)(2,1)} copy(bf16[256,128]{1,0:T(8,128)(2,1)} %get-tuple-element.4) | data formatting | bytes 131072
  49.6 0.0 copy-done
  49.6 0.5 %copy.21 = bf16[1,128]{1,0:T(2,128)(2,1)} copy(bf16[1,128]{1,0:T(2,128)(2,1)S(1)} %copy-done) | data formatting | bytes 512
Async XLA Ops:
  48.2 1.5 %copy-start = (bf16[1,128]{1,0:T(2,128)(2,1)S(1)}, bf16[1,128]{1,0:T(2,128)(2,1)}, u32[]{:S(2)}) copy-start(bf16[1,128]{1,0:T(2,128)(2,1)} %get-tuple-element.5) | copy-start | bytes 772
